TPU v7x, 32 devices: a whole 2x2x4 slice. The times are simulated.
32 devices in a mesh: tm: 4 (over z), space: 8 (over y, x, core).
Axes of the slice: x: 2, y: 2, z: 4, core: 2. Of those that a mesh axis runs over, the one named last changes fastest.
Arguments:
- snapshots: bfloat16 [512, 393216], P('tm', 'space'), may hold values from -10 to 10, as said below
- area_weight: float32 [393216], P('space'), may hold values from 0.1 to 1
- eigvecs: bfloat16 [512, 64], replicated, may hold values from -0.25 to 0.25
- eigvals: float32 [64], replicated, may hold values from 0.5 to 8
Outputs:
- gram: float32 [512, 512], P(('tm', 'space'))
- modes: bfloat16 [64, 393216], P('tm', 'space')
Inputs may be any that keep to these rules, and one draw needn't show every extreme that they name: `snapshots`: a per-column climatology plus hourly departures.
All inputs are finite; a program needn't handle non-finite values.
Results may differ from a plain program's by a relative error of at most 0.01.
Values may be sent and summed in bfloat16 or wider, within the bound.
No kernel may reach another device: no remote copies, remote signals or barrier semaphores. Data moves between devices by JAX's collectives and lax.ppermute only.
A program may use at most 128 MiB of HBM per device.

v0:
```python
import functools
import jax
import jax.numpy as jnp
from jax import lax
from jax.experimental import pallas as pl
from jax.experimental.pallas import tpu as pltpu
from jax.sharding import PartitionSpec as P

SHARES = (1, 8, 2, 1)
GROUPS = (0, 0, 1, 1)


def partner_table(count):
    if count & (count - 1) == 0:
        return lambda i, s: i ^ s, lambda i, s: i ^ s
    return lambda i, s: (i + s) % count, lambda i, s: (i - s) % count


def chunk_tiles(total):
    whole = sum(SHARES)
    ends = [round(total * sum(SHARES[: n + 1]) / whole) for n in range(len(SHARES))]
    starts = [0] + ends[:-1]
    return [(a, b, g) for a, b, g in zip(starts, ends, GROUPS) if b > a]


def tile_of(sub):
    return next((t for t in (1024, 512, 256) if sub % t == 0 and sub // t >= sum(SHARES)), 128)


def chunk_kernel(
    times, time_dev, count, first, last, carried, scale, source, where_ref, own_ref, *refs
):
    recv_refs, refs = refs[: count - 1], refs[count - 1 :]
    root_ref, eig_ref, inv_ref = refs[:3]
    refs = refs[3:]
    if not first:
        prev_ref, refs = refs[0], refs[1:]
    refs = refs[carried:]
    mode_refs, refs = refs[:count], refs[count:]
    gram_ref, refs = refs[0], refs[1:]
    weighted, refs = refs[0], refs[1:]
    total = refs[0] if last else gram_ref
    step = pl.program_id(0)
    me = where_ref[0]
    width = own_ref.shape[1]
    rows = 16

    @pl.when(step == 0)
    def _():
        total[...] = jnp.zeros_like(total) if first else prev_ref[...]

    blocks = (own_ref,) + tuple(recv_refs)
    sums = jnp.zeros((rows, width), jnp.float32)
    for block in blocks:
        for r in range(0, time_dev, rows):
            sums = sums + block[r : r + rows, :].astype(jnp.float32)
    mean = jnp.sum(sums, axis=0, keepdims=True) / times
    root = root_ref[...]
    for s, block in enumerate(blocks):
        base = source(me, s) * time_dev
        for r in range(0, time_dev, rows):
            centred = block[r : r + rows, :].astype(jnp.float32) - mean
            weighted[pl.ds(pl.multiple_of(base + r, rows), rows), :] = (root * centred).astype(
                jnp.bfloat16
            )
    values = weighted[...]
    total[...] += lax.dot_general(
        values, values, (((1,), (1,)), ((), ())), preferred_element_type=jnp.float32
    )
    projected = jnp.dot(eig_ref[...], values, preferred_element_type=jnp.float32) * inv_ref[...]
    depth = mode_refs[0].shape[0]
    for s, mode_ref in enumerate(mode_refs):
        mode_ref[...] = projected[s * depth : (s + 1) * depth, :].astype(jnp.bfloat16)

    if last:

        @pl.when(step == pl.num_programs(0) - 1)
        def _():
            space_count, _, _ = gram_ref.shape
            block_rows = times // (space_count * count)
            for s in range(space_count):
                pieces = [
                    total[pl.ds((i * space_count + s) * block_rows, block_rows), :]
                    for i in range(count)
                ]
                gram_ref[s] = (jnp.concatenate(pieces, axis=0) * scale).astype(jnp.bfloat16)


def run_chunk(
    snapshots, recv, root, eig, inv, prev, modes, where, span, group, tile, last, space_count, source
):
    lo, hi = span
    group_lo, group_hi = group
    time_dev = snapshots.shape[0]
    count = len(recv) + 1
    times = time_dev * count
    steps = hi - lo
    depth = eig.shape[0] // count
    first = prev is None
    cells = snapshots.shape[1] * space_count
    kernel = functools.partial(
        chunk_kernel, times, time_dev, count, first, last, len(modes), 1.0 / cells, source
    )
    in_specs = [pl.BlockSpec((time_dev, tile), lambda g, w: (0, w[1] + lo + g))]
    in_specs += [pl.BlockSpec((time_dev, tile), lambda g, w: (0, g))] * (count - 1)
    in_specs += [
        pl.BlockSpec((1, tile), lambda g, w: (0, lo + g)),
        pl.BlockSpec(eig.shape, lambda g, w: (0, 0)),
        pl.BlockSpec(inv.shape, lambda g, w: (0, 0)),
    ]
    operands = [snapshots, *recv, root, eig, inv]
    if not first:
        in_specs.append(pl.BlockSpec((times, times), lambda g, w: (0, 0)))
        operands.append(prev)
    aliases = {len(operands) + 1 + n: n for n in range(len(modes))}
    in_specs += [pl.BlockSpec(memory_space=pl.ANY)] * len(modes)
    operands += modes
    out_specs = [pl.BlockSpec((depth, tile), lambda g, w: (0, lo - group_lo + g))] * count
    out_shape = [jax.ShapeDtypeStruct((depth, (group_hi - group_lo) * tile), jnp.bfloat16)] * count
    scratch = [pltpu.VMEM((times, tile), jnp.bfloat16)]
    if last:
        shape = (space_count, times // space_count, times)
        out_specs.append(pl.BlockSpec(shape, lambda g, w: (0, 0, 0)))
        out_shape.append(jax.ShapeDtypeStruct(shape, jnp.bfloat16))
        scratch.append(pltpu.VMEM((times, times), jnp.float32))
    else:
        out_specs.append(pl.BlockSpec((times, times), lambda g, w: (0, 0)))
        out_shape.append(jax.ShapeDtypeStruct((times, times), jnp.float32))
    columns = steps * tile
    cost = pl.CostEstimate(
        flops=2 * times * (times + eig.shape[0]) * columns,
        bytes_accessed=2 * times * columns + 8 * times * times,
        transcendentals=0,
    )
    out = pl.pallas_call(
        kernel,
        out_shape=out_shape,
        grid_spec=pltpu.PrefetchScalarGridSpec(
            num_scalar_prefetch=1,
            grid=(steps,),
            in_specs=in_specs,
            out_specs=out_specs,
            scratch_shapes=scratch,
        ),
        input_output_aliases=aliases,
        cost_estimate=cost,
        name="chunk_last" if last else "chunk",
    )(where, *operands)
    return out[:count], out[count]


def local(snapshots, area_weight, eigvecs, eigvals):
    count = lax.axis_size("tm")
    space_count = lax.axis_size("space")
    me = lax.axis_index("tm")
    _, cell_dev = snapshots.shape
    sub = cell_dev // count
    depth = eigvals.shape[0] // count
    tile = tile_of(sub)
    tiles = sub // tile
    chunks = chunk_tiles(tiles)
    target, source = partner_table(count)

    def permute(piece, s):
        return lax.ppermute(piece, "tm", [(i, target(i, s)) for i in range(count)])

    received = []
    for lo, hi, _ in chunks:
        pieces = []
        for s in range(1, count):
            start = target(me, s) * sub + lo * tile
            piece = lax.dynamic_slice_in_dim(snapshots, start, (hi - lo) * tile, 1)
            pieces.append(permute(piece, s))
        received.append(pieces)

    own_weight = lax.dynamic_slice_in_dim(area_weight, me * sub, sub, 0)
    root = jnp.sqrt(own_weight)[None, :]
    eig_rows = eigvecs.T
    inv_rows = (1.0 / jnp.sqrt(eigvals))[:, None]
    order = [target(me, s) * depth for s in range(count)]
    eig = jnp.concatenate([lax.dynamic_slice_in_dim(eig_rows, o, depth, 0) for o in order], axis=0)
    inv = jnp.concatenate([lax.dynamic_slice_in_dim(inv_rows, o, depth, 0) for o in order], axis=0)
    where = jnp.stack([me, me * tiles]).astype(jnp.int32)

    gram = None
    groups = {}
    for n, (lo, hi, group) in enumerate(chunks):
        last = n == len(chunks) - 1
        members = [c for c in chunks if c[2] == group]
        bounds = (members[0][0], members[-1][1])
        pieces = groups[group][1] if group in groups else []
        pieces, gram = run_chunk(
            snapshots, received[n], root, eig, inv, gram, pieces, where,
            (lo, hi), bounds, tile, last, space_count, source,
        )
        groups[group] = (bounds[0], pieces)

    rows = gram.shape[1] // count
    parts = lax.all_to_all(gram, "space", split_axis=0, concat_axis=0, tiled=True)
    row_sums = jnp.sum(parts.astype(jnp.float32), axis=0).astype(jnp.bfloat16)
    row_sums = row_sums.reshape(count, rows, gram.shape[2])
    parts = lax.all_to_all(row_sums, "tm", split_axis=0, concat_axis=0, tiled=True)
    gram_rows = jnp.sum(parts.astype(jnp.float32), axis=0)

    modes = jnp.zeros((depth, cell_dev), jnp.bfloat16)
    modes, _ = lax.optimization_barrier((modes, row_sums))
    for (lo, pieces) in groups.values():
        for s, piece in enumerate(pieces):
            if s > 0:
                piece = permute(piece, s)
            modes = lax.dynamic_update_slice_in_dim(
                modes, piece, source(me, s) * sub + lo * tile, 1
            )
    return gram_rows, modes


def solution(mesh):
    in_specs = (P("tm", "space"), P("space"), P(), P())
    out_specs = (P(("tm", "space"), None), P("tm", "space"))

    return jax.shard_map(local, mesh=mesh, in_specs=in_specs, out_specs=out_specs, check_vma=False)
```

profile of v0, /device:TPU:0, one launch (start us, length us, event | category | flops | bytes accessed | tf_op | source)
XLA Modules:
  0.0 344.0 jit_solution(10669199270463470283)
XLA Ops:
  0.7 5.5 %constant_dynamic-slice_fusion.3 = (bf16[128,8192]{1,0:T(8,128)(2,1)S(1)}, bf16[128,8192]{1,0:T(8,128)(2,1)}, bf16[128,8192]{1,0:T(8,128)(2,1)}) fusion(bf16[128,49152]{1,0:T(8,128)(2,1)} %own_ref.7, s32[]{:T(128)S(6)} %select_n.78, s32[]{:T(128)S(6)} %select_n.77, s32[]{:T(128)S(6)} %select_n.76), kind=kLoop, calls=%fused_computation.18 | loop fusion | bytes 12582924 | tf_op jit(solution)/shard_map/dynamic_slice | solution.py:172
  6.2 3.1 collective-permute-start.6
  9.3 2.6 collective-permute-start.7
  11.8 2.4 constant_dynamic-slice_fusion
  14.3 1.9 collective-permute-start.10
  16.2 1.9 collective-permute-start.11
  18.1 2.3 constant_dynamic-slice_fusion.6
  20.4 190.2 %collective-permute-done.10.refs_1_ = bf16[128,1024]{1,0:T(8,128)(2,1)} collective-permute-done((bf16[128,1024]{1,0:T(8,128)(2,1)}, bf16[128,1024]{1,0:T(8,128)(2,1)}, u32[]{:S(2)}, u32[]{:S(2)}) %collective-permute-start.10) | collective-permute-done | bytes 262176 | tf_op jit(solution)/shard_map/ppermute | solution.py:165
  211.4 4.1 %collective-permute-start.9 = (bf16[128,1024]{1,0:T(8,128)(2,1)}, bf16[128,1024]{1,0:T(8,128)(2,1)}, u32[]{:S(2)}, u32[]{:S(2)}) collective-permute-start(bf16[128,1024]{1,0:T(8,128)(2,1)} %get-tuple-element.46), channel_id=1, source_target_pairs={{0,8},{8,0},{16,24},{24,16},{1,9},{9,1},{17,25},{25,17},{2,10},{10... | collective-permute-start | bytes 786440 | tf_op jit(solution)/shard_map/ppermute | solution.py:165
  217.5 10.3 %collective-permute-done.9.refs_0_ = bf16[128,1024]{1,0:T(8,128)(2,1)} collective-permute-done((bf16[128,1024]{1,0:T(8,128)(2,1)}, bf16[128,1024]{1,0:T(8,128)(2,1)}, u32[]{:S(2)}, u32[]{:S(2)}) %collective-permute-start.9) | collective-permute-done | bytes 262176 | tf_op jit(solution)/shard_map/ppermute | solution.py:165
  231.2 4.1 %chunk.3 = (bf16[16,9216]{1,0:T(8,128)(2,1)}, bf16[16,9216]{1,0:T(8,128)(2,1)}, bf16[16,9216]{1,0:T(8,128)(2,1)}, bf16[16,9216]{1,0:T(8,128)(2,1)}, f32[512,512]{1,0:T(8,128)}) custom-call(s32[2]{0:T(128)} %pad_add_fusion.where_ref, bf16[128,49152]{1,0:T(8,128)(2,1)} %own_ref.7, bf16[128,1024]{1,0:T(8,128)(2,1)} %collective-permute-done.9.refs_0_, ...), custom_call_target="tpu_custom_call" | custom-call | flops 603979776 | bytes 3145728 | tf_op jit(solution)/shard_map/chunk/pallas_call | solution.py:135
  236.2 2.8 collective-permute-start.1
  239.8 14.0 %chunk.4 = (bf16[16,9216]{1,0:T(8,128)(2,1)}, bf16[16,9216]{1,0:T(8,128)(2,1)}, bf16[16,9216]{1,0:T(8,128)(2,1)}, bf16[16,9216]{1,0:T(8,128)(2,1)}, f32[512,512]{1,0:T(8,128)}) custom-call(s32[2]{0:T(128)} %pad_add_fusion.where_ref, bf16[128,49152]{1,0:T(8,128)(2,1)} %own_ref.7, ...), custom_call_target="tpu_custom_call", output_to_operand_aliasing={{0}: (9, {}), {1}: (10, {}), {2}: (11, {}), {3}: (12, {})} | custom-call | flops 4831838208 | bytes 10485760 | tf_op jit(solution)/shard_map/chunk/pallas_call | solution.py:135
  253.8 19.8 %collective-permute-done.4.refs_1_ = bf16[128,2048]{1,0:T(8,128)(2,1)} collective-permute-done((bf16[128,2048]{1,0:T(8,128)(2,1)S(1)}, bf16[128,2048]{1,0:T(8,128)(2,1)}, u32[]{:S(2)}, u32[]{:S(2)}) %collective-permute-start.4) | collective-permute-done | bytes 524320 | tf_op jit(solution)/shard_map/ppermute | solution.py:165
  273.6 6.0 %chunk.5 = (bf16[16,3072]{1,0:T(8,128)(2,1)}, bf16[16,3072]{1,0:T(8,128)(2,1)}, bf16[16,3072]{1,0:T(8,128)(2,1)}, bf16[16,3072]{1,0:T(8,128)(2,1)}, f32[512,512]{1,0:T(8,128)}) custom-call(s32[2]{0:T(128)} %pad_add_fusion.where_ref, bf16[128,49152]{1,0:T(8,128)(2,1)} %own_ref.7, bf16[128,2048]{1,0:T(8,128)(2,1)} %collective-permute-done.3.refs_0_, ...), custom_call_target="tpu_custom_call" | custom-call | flops 1207959552 | bytes 4194304 | tf_op jit(solution)/shard_map/chunk/pallas_call | solution.py:135
  279.6 10.9 %collective-permute-done.1.refs_1_ = bf16[128,1024]{1,0:T(8,128)(2,1)} collective-permute-done((bf16[128,1024]{1,0:T(8,128)(2,1)}, bf16[128,1024]{1,0:T(8,128)(2,1)}, u32[]{:S(2)}, u32[]{:S(2)}) %collective-permute-start.1) | collective-permute-done | bytes 262176 | tf_op jit(solution)/shard_map/ppermute | solution.py:165
  291.2 4.5 %chunk_last.1 = (bf16[16,3072]{1,0:T(8,128)(2,1)}, bf16[16,3072]{1,0:T(8,128)(2,1)}, bf16[16,3072]{1,0:T(8,128)(2,1)}, bf16[16,3072]{1,0:T(8,128)(2,1)}, bf16[8,64,512]{2,1,0:T(8,128)(2,1)}) custom-call(s32[2]{0:T(128)} %pad_add_fusion.where_ref, ...), custom_call_target="tpu_custom_call", output_to_operand_aliasing={{0}: (9, {}), {1}: (10, {}), {2}: (11, {}), {3}: (12, {})} | custom-call | flops 603979776 | bytes 3145728 | tf_op jit(solution)/shard_map/chunk_last/pallas_call | solution.py:135
  295.7 3.9 %all-to-all-start = ((bf16[8,64,512]{2,1,0:T(8,128)(2,1)}), bf16[8,64,512]{2,1,0:T(8,128)(2,1)S(1)}, u32[]{:S(2)}, u32[]{:S(2)}) async-start(bf16[8,64,512]{2,1,0:T(8,128)(2,1)} %get-tuple-element.34), calls=%async_computation | async-start | bytes 1048576 | tf_op jit(solution)/shard_map/all_to_all | solution.py:199
  299.6 5.4 %collective-permute-start.12 = (bf16[16,9216]{1,0:T(8,128)(2,1)S(1)}, bf16[16,9216]{1,0:T(8,128)(2,1)S(1)}, u32[]{:S(2)}, u32[]{:S(2)}) collective-permute-start(bf16[16,9216]{1,0:T(8,128)(2,1)S(1)} %copy-done.3), channel_id=1, source_target_pairs={{0,8},{8,0},{16,24},{24,16},{1,9},{9,1},{17,25},{25,17},{2,10},{10... | collective-permute-start | bytes 884744 | tf_op jit(solution)/shard_map/ppermute | solution.py:165
  308.5 2.0 collective-permute-start.16
  311.2 6.4 %all-to-all-start.1 = ((bf16[4,16,512]{2,1,0:T(8,128)(2,1)}), bf16[4,16,512]{2,1,0:T(8,128)(2,1)S(1)}, u32[]{:S(2)}, u32[]{:S(2)}) async-start(bf16[4,16,512]{2,1,0:T(8,128)(2,1)} %bitcast.11), calls=%async_computation.1 | async-start | bytes 131072 | tf_op jit(solution)/shard_map/all_to_all | solution.py:202
  318.7 2.9 collective-permute-start.17
  321.7 6.7 %collective-permute-done.13 = bf16[16,9216]{1,0:T(8,128)(2,1)S(1)} collective-permute-done((bf16[16,9216]{1,0:T(8,128)(2,1)S(1)}, bf16[16,9216]{1,0:T(8,128)(2,1)S(1)}, u32[]{:S(2)}, u32[]{:S(2)}) %collective-permute-start.13) | collective-permute-done | bytes 294944 | tf_op jit(solution)/shard_map/ppermute | solution.py:165
  329.5 12.4 %collective-permute-done.16 = bf16[16,3072]{1,0:T(8,128)(2,1)} collective-permute-done((bf16[16,3072]{1,0:T(8,128)(2,1)}, bf16[16,3072]{1,0:T(8,128)(2,1)}, u32[]{:S(2)}, u32[]{:S(2)}) %collective-permute-start.16) | collective-permute-done | bytes 98336 | tf_op jit(solution)/shard_map/ppermute | solution.py:165
  (60 shorter events, 16.9 us)
Async XLA Ops:
  6.2 229.2 %collective-permute-start.6 = (bf16[128,8192]{1,0:T(8,128)(2,1)}, bf16[128,8192]{1,0:T(8,128)(2,1)}, u32[]{:S(2)}, u32[]{:S(2)}) collective-permute-start(bf16[128,8192]{1,0:T(8,128)(2,1)} %get-tuple-element.52), channel_id=1, source_target_pairs={{0,8},{8,0},{16,24},{24,16},{1,9},{9,1},{17,25},{25,17},{2,10},{10... | collective-permute-start | bytes 6291464 | tf_op jit(solution)/shard_map/ppermute | solution.py:165
  9.3 227.0 %collective-permute-start.7 = (bf16[128,8192]{1,0:T(8,128)(2,1)}, bf16[128,8192]{1,0:T(8,128)(2,1)}, u32[]{:S(2)}, u32[]{:S(2)}) collective-permute-start(bf16[128,8192]{1,0:T(8,128)(2,1)} %get-tuple-element.51), channel_id=1, source_target_pairs={{0,16},{8,24},{16,0},{24,8},{1,17},{9,25},{17,1},{25,9},{2,18},{10... | collective-permute-start | bytes 6291464 | tf_op jit(solution)/shard_map/ppermute | solution.py:165
  11.8 227.2 %collective-permute-start.8 = (bf16[128,8192]{1,0:T(8,128)(2,1)S(1)}, bf16[128,8192]{1,0:T(8,128)(2,1)}, u32[]{:S(2)}, u32[]{:S(2)}) collective-permute-start(bf16[128,8192]{1,0:T(8,128)(2,1)S(1)} %get-tuple-element.50), channel_id=1, source_target_pairs={{0,24},{8,16},{16,8},{24,0},{1,25},{9,17},{17,9},{25,1},{2,26},{10... | collective-permute-start | bytes 6291464 | tf_op jit(solution)/shard_map/ppermute | solution.py:165
  14.3 196.4 %collective-permute-start.10 = (bf16[128,1024]{1,0:T(8,128)(2,1)}, bf16[128,1024]{1,0:T(8,128)(2,1)}, u32[]{:S(2)}, u32[]{:S(2)}) collective-permute-start(bf16[128,1024]{1,0:T(8,128)(2,1)} %get-tuple-element.45), channel_id=1, source_target_pairs={{0,16},{8,24},{16,0},{24,8},{1,17},{9,25},{17,1},{25,9},{2,18},{10... | collective-permute-start | bytes 786440 | tf_op jit(solution)/shard_map/ppermute | solution.py:165
  16.2 195.2 %collective-permute-start.11 = (bf16[128,1024]{1,0:T(8,128)(2,1)}, bf16[128,1024]{1,0:T(8,128)(2,1)}, u32[]{:S(2)}, u32[]{:S(2)}) collective-permute-start(bf16[128,1024]{1,0:T(8,128)(2,1)} %get-tuple-element.44), channel_id=1, source_target_pairs={{0,24},{8,16},{16,8},{24,0},{1,25},{9,17},{17,9},{25,1},{2,26},{10... | collective-permute-start | bytes 786440 | tf_op jit(solution)/shard_map/ppermute | solution.py:165
  210.6 19.0 %collective-permute-start.3 = (bf16[128,2048]{1,0:T(8,128)(2,1)}, bf16[128,2048]{1,0:T(8,128)(2,1)}, u32[]{:S(2)}, u32[]{:S(2)}) collective-permute-start(bf16[128,2048]{1,0:T(8,128)(2,1)} %get-tuple-element.55), channel_id=1, source_target_pairs={{0,8},{8,0},{16,24},{24,16},{1,9},{9,1},{17,25},{25,17},{2,10},{10... | collective-permute-start | bytes 1572872 | tf_op jit(solution)/shard_map/ppermute | solution.py:165
  211.4 16.4 %collective-permute-start.9 = (bf16[128,1024]{1,0:T(8,128)(2,1)}, bf16[128,1024]{1,0:T(8,128)(2,1)}, u32[]{:S(2)}, u32[]{:S(2)}) collective-permute-start(bf16[128,1024]{1,0:T(8,128)(2,1)} %get-tuple-element.46), channel_id=1, source_target_pairs={{0,8},{8,0},{16,24},{24,16},{1,9},{9,1},{17,25},{25,17},{2,10},{10... | collective-permute-start | bytes 786440 | tf_op jit(solution)/shard_map/ppermute | solution.py:165
  227.8 45.8 %collective-permute-start.4 = (bf16[128,2048]{1,0:T(8,128)(2,1)S(1)}, bf16[128,2048]{1,0:T(8,128)(2,1)}, u32[]{:S(2)}, u32[]{:S(2)}) collective-permute-start(bf16[128,2048]{1,0:T(8,128)(2,1)S(1)} %get-tuple-element.54), channel_id=1, source_target_pairs={{0,16},{8,24},{16,0},{24,8},{1,17},{9,25},{17,1},{25,9},{2,18},{10... | collective-permute-start | bytes 1572872 | tf_op jit(solution)/shard_map/ppermute | solution.py:165
  229.7 43.9 %collective-permute-start.5 = (bf16[128,2048]{1,0:T(8,128)(2,1)S(1)}, bf16[128,2048]{1,0:T(8,128)(2,1)}, u32[]{:S(2)}, u32[]{:S(2)}) collective-permute-start(bf16[128,2048]{1,0:T(8,128)(2,1)S(1)} %get-tuple-element.53), channel_id=1, source_target_pairs={{0,24},{8,16},{16,8},{24,0},{1,25},{9,17},{17,9},{25,1},{2,26},{10... | collective-permute-start | bytes 1572872 | tf_op jit(solution)/shard_map/ppermute | solution.py:165
  235.4 44.2 %collective-permute-start = (bf16[128,1024]{1,0:T(8,128)(2,1)}, bf16[128,1024]{1,0:T(8,128)(2,1)}, u32[]{:S(2)}, u32[]{:S(2)}) collective-permute-start(bf16[128,1024]{1,0:T(8,128)(2,1)} %get-tuple-element.49), channel_id=1, source_target_pairs={{0,8},{8,0},{16,24},{24,16},{1,9},{9,1},{17,25},{25,17},{2,10},{10... | collective-permute-start | bytes 786440 | tf_op jit(solution)/shard_map/ppermute | solution.py:165
  236.2 54.2 %collective-permute-start.1 = (bf16[128,1024]{1,0:T(8,128)(2,1)}, bf16[128,1024]{1,0:T(8,128)(2,1)}, u32[]{:S(2)}, u32[]{:S(2)}) collective-permute-start(bf16[128,1024]{1,0:T(8,128)(2,1)} %get-tuple-element.48), channel_id=1, source_target_pairs={{0,16},{8,24},{16,0},{24,8},{1,17},{9,25},{17,1},{25,9},{2,18},{10... | collective-permute-start | bytes 786440 | tf_op jit(solution)/shard_map/ppermute | solution.py:165
  239.0 51.4 %collective-permute-start.2 = (bf16[128,1024]{1,0:T(8,128)(2,1)S(1)}, bf16[128,1024]{1,0:T(8,128)(2,1)S(1)}, u32[]{:S(2)}, u32[]{:S(2)}) collective-permute-start(bf16[128,1024]{1,0:T(8,128)(2,1)S(1)} %get-tuple-element.47), channel_id=1, source_target_pairs={{0,24},{8,16},{16,8},{24,0},{1,25},{9,17},{17,9},{25,1},{2,26},{10... | collective-permute-start | bytes 786440 | tf_op jit(solution)/shard_map/ppermute | solution.py:165
  291.2 13.8 %copy-start.4 = (bf16[16,9216]{1,0:T(8,128)(2,1)S(1)}, bf16[16,9216]{1,0:T(8,128)(2,1)}, u32[]{:S(2)}) copy-start(bf16[16,9216]{1,0:T(8,128)(2,1)} %get-tuple-element.38) | copy-start | bytes 884740
  295.7 22.0 %copy-start.1 = (bf16[16,9216]{1,0:T(8,128)(2,1)S(1)}, bf16[16,9216]{1,0:T(8,128)(2,1)}, u32[]{:S(2)}) copy-start(bf16[16,9216]{1,0:T(8,128)(2,1)} %get-tuple-element.36) | copy-start | bytes 884740
  295.7 14.8 %all-to-all-start = ((bf16[8,64,512]{2,1,0:T(8,128)(2,1)}), bf16[8,64,512]{2,1,0:T(8,128)(2,1)S(1)}, u32[]{:S(2)}, u32[]{:S(2)}) async-start(bf16[8,64,512]{2,1,0:T(8,128)(2,1)} %get-tuple-element.34), calls=%async_computation | async-start | bytes 1048576 | tf_op jit(solution)/shard_map/all_to_all | solution.py:199
  299.5 19.2 %copy-start.6 = (bf16[16,3072]{1,0:T(8,128)(2,1)S(1)}, bf16[16,3072]{1,0:T(8,128)(2,1)}, u32[]{:S(2)}) copy-start(bf16[16,3072]{1,0:T(8,128)(2,1)} %get-tuple-element.43) | copy-start | bytes 294916
  299.6 19.2 %collective-permute-start.12 = (bf16[16,9216]{1,0:T(8,128)(2,1)S(1)}, bf16[16,9216]{1,0:T(8,128)(2,1)S(1)}, u32[]{:S(2)}, u32[]{:S(2)}) collective-permute-start(bf16[16,9216]{1,0:T(8,128)(2,1)S(1)} %copy-done.3), channel_id=1, source_target_pairs={{0,8},{8,0},{16,24},{24,16},{1,9},{9,1},{17,25},{25,17},{2,10},{10... | collective-permute-start | bytes 884744 | tf_op jit(solution)/shard_map/ppermute | solution.py:165
  305.0 23.5 %collective-permute-start.13 = (bf16[16,9216]{1,0:T(8,128)(2,1)S(1)}, bf16[16,9216]{1,0:T(8,128)(2,1)S(1)}, u32[]{:S(2)}, u32[]{:S(2)}) collective-permute-start(bf16[16,9216]{1,0:T(8,128)(2,1)S(1)} %copy-done.4), channel_id=1, source_target_pairs={{0,16},{8,24},{16,0},{24,8},{1,17},{9,25},{17,1},{25,9},{2,18},{10... | collective-permute-start | bytes 884744 | tf_op jit(solution)/shard_map/ppermute | solution.py:165
  306.1 22.4 %collective-permute-start.14 = (bf16[16,9216]{1,0:T(8,128)(2,1)}, bf16[16,9216]{1,0:T(8,128)(2,1)S(1)}, u32[]{:S(2)}, u32[]{:S(2)}) collective-permute-start(bf16[16,9216]{1,0:T(8,128)(2,1)} %get-tuple-element.39), channel_id=1, source_target_pairs={{0,24},{8,16},{16,8},{24,0},{1,25},{9,17},{17,9},{25,1},{2,26},{10... | collective-permute-start | bytes 884744 | tf_op jit(solution)/shard_map/ppermute | solution.py:165
  307.5 21.1 %collective-permute-start.15 = (bf16[16,3072]{1,0:T(8,128)(2,1)}, bf16[16,3072]{1,0:T(8,128)(2,1)}, u32[]{:S(2)}, u32[]{:S(2)}) collective-permute-start(bf16[16,3072]{1,0:T(8,128)(2,1)} %get-tuple-element.41), channel_id=1, source_target_pairs={{0,8},{8,0},{16,24},{24,16},{1,9},{9,1},{17,25},{25,17},{2,10},{10... | collective-permute-start | bytes 294920 | tf_op jit(solution)/shard_map/ppermute | solution.py:165
  308.5 33.4 %collective-permute-start.16 = (bf16[16,3072]{1,0:T(8,128)(2,1)}, bf16[16,3072]{1,0:T(8,128)(2,1)}, u32[]{:S(2)}, u32[]{:S(2)}) collective-permute-start(bf16[16,3072]{1,0:T(8,128)(2,1)} %get-tuple-element.42), channel_id=1, source_target_pairs={{0,16},{8,24},{16,0},{24,8},{1,17},{9,25},{17,1},{25,9},{2,18},{10... | collective-permute-start | bytes 294920 | tf_op jit(solution)/shard_map/ppermute | solution.py:165
  311.2 31.7 %all-to-all-start.1 = ((bf16[4,16,512]{2,1,0:T(8,128)(2,1)}), bf16[4,16,512]{2,1,0:T(8,128)(2,1)S(1)}, u32[]{:S(2)}, u32[]{:S(2)}) async-start(bf16[4,16,512]{2,1,0:T(8,128)(2,1)} %bitcast.11), calls=%async_computation.1 | async-start | bytes 131072 | tf_op jit(solution)/shard_map/all_to_all | solution.py:202
  317.7 10.8 %copy-start.2 = (bf16[16,3072]{1,0:T(8,128)(2,1)S(1)}, bf16[16,3072]{1,0:T(8,128)(2,1)}, u32[]{:S(2)}) copy-start(bf16[16,3072]{1,0:T(8,128)(2,1)} %get-tuple-element.40) | copy-start | bytes 294916
  318.7 24.1 %collective-permute-start.17 = (bf16[16,3072]{1,0:T(8,128)(2,1)S(1)}, bf16[16,3072]{1,0:T(8,128)(2,1)S(1)}, u32[]{:S(2)}, u32[]{:S(2)}) collective-permute-start(bf16[16,3072]{1,0:T(8,128)(2,1)S(1)} %copy-done.6), channel_id=1, source_target_pairs={{0,24},{8,16},{16,8},{24,0},{1,25},{9,17},{17,9},{25,1},{2,26},{10... | collective-permute-start | bytes 294920 | tf_op jit(solution)/shard_map/ppermute | solution.py:165
  (5 other events, 14.9 us)
where the time goes:
time: 345 us; the launch traced here: 344 us
  waiting for transfers between devices  251 us (73%)
  starting transfers between devices  44.7 us (13%)
  Pallas kernels  28.6 us (8%)
  local copies, waits for them, and re-layouts  15.8 us (5%)
    ppermute x18, waiting for transfers between devices, permute(): return lax.ppermute(piece, 'tm', [(i, target(i, s)) for i in range(count)])  251 us
    ppermute x18, starting transfers between devices, permute(): return lax.ppermute(piece, 'tm', [(i, target(i, s)) for i in range(count)])  34.5 us
    pallas_call x4, Pallas kernels, run_chunk(): pl.pallas_call(kernel, out_shape=out_shape, grid_spec=pltpu.PrefetchScala...  28.6 us
    dynamic_slice x3, local copies, waits for them, and re-layouts, local(): piece = lax.dynamic_slice_in_dim(snapshots, start, (hi - lo) * tile, 1)  10.3 us
  transfers between devices with their start and end apart: 20, of which 7 were waited for; matrix products, arithmetic and copies ran while one was open for 3% of the time, Pallas kernels for 7%

commit v1 on v0

--- a/solution.py
+++ b/solution.py
@@ -165,13 +165,16 @@
         return lax.ppermute(piece, "tm", [(i, target(i, s)) for i in range(count)])
 
     received = []
-    for lo, hi, _ in chunks:
-        pieces = []
-        for s in range(1, count):
+    base = snapshots
+    for n, (lo, hi, _) in enumerate(chunks):
+        pieces = {}
+        for s in reversed(range(1, count)):
             start = target(me, s) * sub + lo * tile
-            piece = lax.dynamic_slice_in_dim(snapshots, start, (hi - lo) * tile, 1)
-            pieces.append(permute(piece, s))
-        received.append(pieces)
+            piece = lax.dynamic_slice_in_dim(base, start, (hi - lo) * tile, 1)
+            if n == 0:
+                base, piece = lax.optimization_barrier((base, piece))
+            pieces[s] = permute(piece, s)
+        received.append([pieces[s] for s in range(1, count)])
 
     own_weight = lax.dynamic_slice_in_dim(area_weight, me * sub, sub, 0)
     root = jnp.sqrt(own_weight)[None, :]

time: 345 us -> 337 us (0.977)
  waiting for transfers between devices: 251 us -> 236 us
  local copies, waits for them, and re-layouts: 15.8 us -> 19.6 us
  starting transfers between devices: 44.7 us -> 48.2 us
    ppermute x18, waiting for transfers between devices: 251 us -> 236 us  [permute(): return lax.ppermute(piece, 'tm', [(i, target(i, s)) for i in range(count)])]
    dynamic_slice x3 -> x6, local copies, waits for them, and re-layouts: 10.3 us -> 14.1 us  [local(): piece = lax.dynamic_slice_in_dim(base, start, (hi - lo) * tile, 1)]
  transfers between devices with their start and end apart: 20 -> 20, of which waited for: 7 -> 8; matrix products, arithmetic and copies ran while one was open for 3% -> 3% of each run, Pallas kernels for 7% -> 7%
where the time goes in v1:
time: 337 us; the launch traced here: 336 us
  waiting for transfers between devices  236 us (70%)
  starting transfers between devices  48.2 us (14%)
  Pallas kernels  28.6 us (8%)
  local copies, waits for them, and re-layouts  19.6 us (6%)
    ppermute x18, waiting for transfers between devices, permute(): return lax.ppermute(piece, 'tm', [(i, target(i, s)) for i in range(count)])  236 us
    ppermute x18, starting transfers between devices, permute(): return lax.ppermute(piece, 'tm', [(i, target(i, s)) for i in range(count)])  37.9 us
    pallas_call x4, Pallas kernels, run_chunk(): pl.pallas_call(kernel, out_shape=out_shape, grid_spec=pltpu.PrefetchScala...  28.6 us
    dynamic_slice x6, local copies, waits for them, and re-layouts, local(): piece = lax.dynamic_slice_in_dim(base, start, (hi - lo) * tile, 1)  14.1 us
  transfers between devices with their start and end apart: 20, of which 8 were waited for; matrix products, arithmetic and copies ran while one was open for 3% of the time, Pallas kernels for 7%

profile of v1, /device:TPU:0, one launch (start us, length us, event | category | flops | bytes accessed | tf_op | source)
XLA Modules:
  0.0 336.2 jit_solution(9736628435812691596)
XLA Ops:
  5.0 5.5 %constant_dynamic-slice_fusion = (bf16[128,8192]{1,0:T(8,128)(2,1)S(1)}, bf16[128,8192]{1,0:T(8,128)(2,1)}, bf16[128,8192]{1,0:T(8,128)(2,1)}) fusion(bf16[128,49152]{1,0:T(8,128)(2,1)} %own_ref.7, s32[]{:T(128)S(6)} %select_n.81, s32[]{:T(128)S(6)} %select_n.80, s32[]{:T(128)S(6)} %select_n.79), kind=kLoop, calls=%fused_computation.15 | loop fusion | bytes 12582924 | tf_op jit(solution)/shard_map/dynamic_slice | solution.py:173
  10.5 3.1 collective-permute-start.6
  13.6 2.6 collective-permute-start.7
  17.1 3.5 %collective-permute-start.10 = (bf16[128,1024]{1,0:T(8,128)(2,1)}, bf16[128,1024]{1,0:T(8,128)(2,1)}, u32[]{:S(2)}, u32[]{:S(2)}) collective-permute-start(bf16[128,1024]{1,0:T(8,128)(2,1)} %constant_dynamic-slice_fusion.10), channel_id=1, source_target_pairs={{0,16},{8,24},{16,0},{24,8},{1,17},{9,25},{17,1},{25,9},{2,18},{10... | collective-permute-start | bytes 786440 | tf_op jit(solution)/shard_map/ppermute | solution.py:165
  20.6 2.3 constant_dynamic-slice_fusion.3
  23.5 131.9 %collective-permute-done.9.refs_0_ = bf16[128,1024]{1,0:T(8,128)(2,1)} collective-permute-done((bf16[128,1024]{1,0:T(8,128)(2,1)S(1)}, bf16[128,1024]{1,0:T(8,128)(2,1)}, u32[]{:S(2)}, u32[]{:S(2)}) %collective-permute-start.9) | collective-permute-done | bytes 262176 | tf_op jit(solution)/shard_map/ppermute | solution.py:165
  155.4 2.6 collective-permute-start.3
  160.0 48.0 %collective-permute-done.10.refs_1_ = bf16[128,1024]{1,0:T(8,128)(2,1)} collective-permute-done((bf16[128,1024]{1,0:T(8,128)(2,1)}, bf16[128,1024]{1,0:T(8,128)(2,1)}, u32[]{:S(2)}, u32[]{:S(2)}) %collective-permute-start.10) | collective-permute-done | bytes 262176 | tf_op jit(solution)/shard_map/ppermute | solution.py:165
  208.0 2.9 collective-permute-start.11
  212.9 4.3 %collective-permute-done.11.refs_2_ = bf16[128,1024]{1,0:T(8,128)(2,1)} collective-permute-done((bf16[128,1024]{1,0:T(8,128)(2,1)}, bf16[128,1024]{1,0:T(8,128)(2,1)}, u32[]{:S(2)}, u32[]{:S(2)}) %collective-permute-start.11) | collective-permute-done | bytes 262176 | tf_op jit(solution)/shard_map/ppermute | solution.py:165
  217.2 4.0 %collective-permute-start.4 = (bf16[128,2048]{1,0:T(8,128)(2,1)S(1)}, bf16[128,2048]{1,0:T(8,128)(2,1)}, u32[]{:S(2)}, u32[]{:S(2)}) collective-permute-start(bf16[128,2048]{1,0:T(8,128)(2,1)S(1)} %get-tuple-element.60), channel_id=1, source_target_pairs={{0,16},{8,24},{16,0},{24,8},{1,17},{9,25},{17,1},{25,9},{2,18},{10... | collective-permute-start | bytes 1572872 | tf_op jit(solution)/shard_map/ppermute | solution.py:165
  223.7 4.1 %chunk.3 = (bf16[16,9216]{1,0:T(8,128)(2,1)}, bf16[16,9216]{1,0:T(8,128)(2,1)}, bf16[16,9216]{1,0:T(8,128)(2,1)}, bf16[16,9216]{1,0:T(8,128)(2,1)}, f32[512,512]{1,0:T(8,128)}) custom-call(s32[2]{0:T(128)} %pad_add_fusion.where_ref, bf16[128,49152]{1,0:T(8,128)(2,1)} %own_ref.7, bf16[128,1024]{1,0:T(8,128)(2,1)} %collective-permute-done.9.refs_0_, ...), custom_call_target="tpu_custom_call" | custom-call | flops 603979776 | bytes 3145728 | tf_op jit(solution)/shard_map/chunk/pallas_call | solution.py:135
  227.9 2.6 collective-permute-start.1
  232.3 14.0 %chunk.4 = (bf16[16,9216]{1,0:T(8,128)(2,1)}, bf16[16,9216]{1,0:T(8,128)(2,1)}, bf16[16,9216]{1,0:T(8,128)(2,1)}, bf16[16,9216]{1,0:T(8,128)(2,1)}, f32[512,512]{1,0:T(8,128)}) custom-call(s32[2]{0:T(128)} %pad_add_fusion.where_ref, bf16[128,49152]{1,0:T(8,128)(2,1)} %own_ref.7, ...), custom_call_target="tpu_custom_call", output_to_operand_aliasing={{0}: (9, {}), {1}: (10, {}), {2}: (11, {}), {3}: (12, {})} | custom-call | flops 4831838208 | bytes 10485760 | tf_op jit(solution)/shard_map/chunk/pallas_call | solution.py:135
  246.3 19.9 %collective-permute-done.4.refs_1_ = bf16[128,2048]{1,0:T(8,128)(2,1)} collective-permute-done((bf16[128,2048]{1,0:T(8,128)(2,1)S(1)}, bf16[128,2048]{1,0:T(8,128)(2,1)}, u32[]{:S(2)}, u32[]{:S(2)}) %collective-permute-start.4) | collective-permute-done | bytes 524320 | tf_op jit(solution)/shard_map/ppermute | solution.py:165
  266.2 6.0 %chunk.5 = (bf16[16,3072]{1,0:T(8,128)(2,1)}, bf16[16,3072]{1,0:T(8,128)(2,1)}, bf16[16,3072]{1,0:T(8,128)(2,1)}, bf16[16,3072]{1,0:T(8,128)(2,1)}, f32[512,512]{1,0:T(8,128)}) custom-call(s32[2]{0:T(128)} %pad_add_fusion.where_ref, bf16[128,49152]{1,0:T(8,128)(2,1)} %own_ref.7, bf16[128,2048]{1,0:T(8,128)(2,1)} %collective-permute-done.3.refs_0_, ...), custom_call_target="tpu_custom_call" | custom-call | flops 1207959552 | bytes 4194304 | tf_op jit(solution)/shard_map/chunk/pallas_call | solution.py:135
  272.2 10.9 %collective-permute-done.1.refs_1_ = bf16[128,1024]{1,0:T(8,128)(2,1)} collective-permute-done((bf16[128,1024]{1,0:T(8,128)(2,1)}, bf16[128,1024]{1,0:T(8,128)(2,1)}, u32[]{:S(2)}, u32[]{:S(2)}) %collective-permute-start.1) | collective-permute-done | bytes 262176 | tf_op jit(solution)/shard_map/ppermute | solution.py:165
  283.8 4.5 %chunk_last.1 = (bf16[16,3072]{1,0:T(8,128)(2,1)}, bf16[16,3072]{1,0:T(8,128)(2,1)}, bf16[16,3072]{1,0:T(8,128)(2,1)}, bf16[16,3072]{1,0:T(8,128)(2,1)}, bf16[8,64,512]{2,1,0:T(8,128)(2,1)}) custom-call(s32[2]{0:T(128)} %pad_add_fusion.where_ref, ...), custom_call_target="tpu_custom_call", output_to_operand_aliasing={{0}: (9, {}), {1}: (10, {}), {2}: (11, {}), {3}: (12, {})} | custom-call | flops 603979776 | bytes 3145728 | tf_op jit(solution)/shard_map/chunk_last/pallas_call | solution.py:135
  288.3 3.9 %all-to-all-start = ((bf16[8,64,512]{2,1,0:T(8,128)(2,1)}), bf16[8,64,512]{2,1,0:T(8,128)(2,1)S(1)}, u32[]{:S(2)}, u32[]{:S(2)}) async-start(bf16[8,64,512]{2,1,0:T(8,128)(2,1)} %get-tuple-element.46), calls=%async_computation | async-start | bytes 1048576 | tf_op jit(solution)/shard_map/all_to_all | solution.py:202
  292.2 5.0 %collective-permute-start.12 = (bf16[16,9216]{1,0:T(8,128)(2,1)S(1)}, bf16[16,9216]{1,0:T(8,128)(2,1)S(1)}, u32[]{:S(2)}, u32[]{:S(2)}) collective-permute-start(bf16[16,9216]{1,0:T(8,128)(2,1)S(1)} %copy-done.3), channel_id=1, source_target_pairs={{0,8},{8,0},{16,24},{24,16},{1,9},{9,1},{17,25},{25,17},{2,10},{10... | collective-permute-start | bytes 884744 | tf_op jit(solution)/shard_map/ppermute | solution.py:165
  302.6 6.4 %all-to-all-start.1 = ((bf16[4,16,512]{2,1,0:T(8,128)(2,1)}), bf16[4,16,512]{2,1,0:T(8,128)(2,1)S(1)}, u32[]{:S(2)}, u32[]{:S(2)}) async-start(bf16[4,16,512]{2,1,0:T(8,128)(2,1)} %bitcast.11), calls=%async_computation.1 | async-start | bytes 131072 | tf_op jit(solution)/shard_map/all_to_all | solution.py:205
  310.4 2.6 collective-permute-start.17
  313.1 7.6 %collective-permute-done.13 = bf16[16,9216]{1,0:T(8,128)(2,1)S(1)} collective-permute-done((bf16[16,9216]{1,0:T(8,128)(2,1)S(1)}, bf16[16,9216]{1,0:T(8,128)(2,1)S(1)}, u32[]{:S(2)}, u32[]{:S(2)}) %collective-permute-start.13) | collective-permute-done | bytes 294944 | tf_op jit(solution)/shard_map/ppermute | solution.py:165
  321.7 12.3 %collective-permute-done.16 = bf16[16,3072]{1,0:T(8,128)(2,1)} collective-permute-done((bf16[16,3072]{1,0:T(8,128)(2,1)}, bf16[16,3072]{1,0:T(8,128)(2,1)}, u32[]{:S(2)}, u32[]{:S(2)}) %collective-permute-start.16) | collective-permute-done | bytes 98336 | tf_op jit(solution)/shard_map/ppermute | solution.py:165
  (63 shorter events, 24.9 us)
Async XLA Ops:
  10.5 217.4 %collective-permute-start.6 = (bf16[128,8192]{1,0:T(8,128)(2,1)}, bf16[128,8192]{1,0:T(8,128)(2,1)}, u32[]{:S(2)}, u32[]{:S(2)}) collective-permute-start(bf16[128,8192]{1,0:T(8,128)(2,1)} %get-tuple-element.58), channel_id=1, source_target_pairs={{0,8},{8,0},{16,24},{24,16},{1,9},{9,1},{17,25},{25,17},{2,10},{10... | collective-permute-start | bytes 6291464 | tf_op jit(solution)/shard_map/ppermute | solution.py:165
  13.6 214.3 %collective-permute-start.7 = (bf16[128,8192]{1,0:T(8,128)(2,1)}, bf16[128,8192]{1,0:T(8,128)(2,1)}, u32[]{:S(2)}, u32[]{:S(2)}) collective-permute-start(bf16[128,8192]{1,0:T(8,128)(2,1)} %get-tuple-element.57), channel_id=1, source_target_pairs={{0,16},{8,24},{16,0},{24,8},{1,17},{9,25},{17,1},{25,9},{2,18},{10... | collective-permute-start | bytes 6291464 | tf_op jit(solution)/shard_map/ppermute | solution.py:165
  16.2 214.3 %collective-permute-start.8 = (bf16[128,8192]{1,0:T(8,128)(2,1)S(1)}, bf16[128,8192]{1,0:T(8,128)(2,1)}, u32[]{:S(2)}, u32[]{:S(2)}) collective-permute-start(bf16[128,8192]{1,0:T(8,128)(2,1)S(1)} %get-tuple-element.56), channel_id=1, source_target_pairs={{0,24},{8,16},{16,8},{24,0},{1,25},{9,17},{17,9},{25,1},{2,26},{10... | collective-permute-start | bytes 6291464 | tf_op jit(solution)/shard_map/ppermute | solution.py:165
  16.2 139.2 %collective-permute-start.9 = (bf16[128,1024]{1,0:T(8,128)(2,1)S(1)}, bf16[128,1024]{1,0:T(8,128)(2,1)}, u32[]{:S(2)}, u32[]{:S(2)}) collective-permute-start(bf16[128,1024]{1,0:T(8,128)(2,1)S(1)} %constant_dynamic-slice_fusion.9), channel_id=1, source_target_pairs={{0,8},{8,0},{16,24},{24,16},{1,9},{9,1},{17,25},{25,17},{2,10},{10... | collective-permute-start | bytes 786440 | tf_op jit(solution)/shard_map/ppermute | solution.py:165
  17.1 191.0 %collective-permute-start.10 = (bf16[128,1024]{1,0:T(8,128)(2,1)}, bf16[128,1024]{1,0:T(8,128)(2,1)}, u32[]{:S(2)}, u32[]{:S(2)}) collective-permute-start(bf16[128,1024]{1,0:T(8,128)(2,1)} %constant_dynamic-slice_fusion.10), channel_id=1, source_target_pairs={{0,16},{8,24},{16,0},{24,8},{1,17},{9,25},{17,1},{25,9},{2,18},{10... | collective-permute-start | bytes 786440 | tf_op jit(solution)/shard_map/ppermute | solution.py:165
  155.4 65.8 %collective-permute-start.3 = (bf16[128,2048]{1,0:T(8,128)(2,1)}, bf16[128,2048]{1,0:T(8,128)(2,1)}, u32[]{:S(2)}, u32[]{:S(2)}) collective-permute-start(bf16[128,2048]{1,0:T(8,128)(2,1)} %get-tuple-element.61), channel_id=1, source_target_pairs={{0,8},{8,0},{16,24},{24,16},{1,9},{9,1},{17,25},{25,17},{2,10},{10... | collective-permute-start | bytes 1572872 | tf_op jit(solution)/shard_map/ppermute | solution.py:165
  208.0 9.2 %collective-permute-start.11 = (bf16[128,1024]{1,0:T(8,128)(2,1)}, bf16[128,1024]{1,0:T(8,128)(2,1)}, u32[]{:S(2)}, u32[]{:S(2)}) collective-permute-start(bf16[128,1024]{1,0:T(8,128)(2,1)} %constant_dynamic-slice_fusion.11), channel_id=1, source_target_pairs={{0,24},{8,16},{16,8},{24,0},{1,25},{9,17},{17,9},{25,1},{2,26},{10... | collective-permute-start | bytes 786440 | tf_op jit(solution)/shard_map/ppermute | solution.py:165
  217.2 49.0 %collective-permute-start.4 = (bf16[128,2048]{1,0:T(8,128)(2,1)S(1)}, bf16[128,2048]{1,0:T(8,128)(2,1)}, u32[]{:S(2)}, u32[]{:S(2)}) collective-permute-start(bf16[128,2048]{1,0:T(8,128)(2,1)S(1)} %get-tuple-element.60), channel_id=1, source_target_pairs={{0,16},{8,24},{16,0},{24,8},{1,17},{9,25},{17,1},{25,9},{2,18},{10... | collective-permute-start | bytes 1572872 | tf_op jit(solution)/shard_map/ppermute | solution.py:165
  221.2 45.0 %collective-permute-start.5 = (bf16[128,2048]{1,0:T(8,128)(2,1)S(1)}, bf16[128,2048]{1,0:T(8,128)(2,1)}, u32[]{:S(2)}, u32[]{:S(2)}) collective-permute-start(bf16[128,2048]{1,0:T(8,128)(2,1)S(1)} %get-tuple-element.59), channel_id=1, source_target_pairs={{0,24},{8,16},{16,8},{24,0},{1,25},{9,17},{17,9},{25,1},{2,26},{10... | collective-permute-start | bytes 1572872 | tf_op jit(solution)/shard_map/ppermute | solution.py:165
  227.9 44.3 %collective-permute-start = (bf16[128,1024]{1,0:T(8,128)(2,1)}, bf16[128,1024]{1,0:T(8,128)(2,1)}, u32[]{:S(2)}, u32[]{:S(2)}) collective-permute-start(bf16[128,1024]{1,0:T(8,128)(2,1)} %get-tuple-element.64), channel_id=1, source_target_pairs={{0,8},{8,0},{16,24},{24,16},{1,9},{9,1},{17,25},{25,17},{2,10},{10... | collective-permute-start | bytes 786440 | tf_op jit(solution)/shard_map/ppermute | solution.py:165
  227.9 55.2 %collective-permute-start.1 = (bf16[128,1024]{1,0:T(8,128)(2,1)}, bf16[128,1024]{1,0:T(8,128)(2,1)}, u32[]{:S(2)}, u32[]{:S(2)}) collective-permute-start(bf16[128,1024]{1,0:T(8,128)(2,1)} %get-tuple-element.63), channel_id=1, source_target_pairs={{0,16},{8,24},{16,0},{24,8},{1,17},{9,25},{17,1},{25,9},{2,18},{10... | collective-permute-start | bytes 786440 | tf_op jit(solution)/shard_map/ppermute | solution.py:165
  230.5 52.5 %collective-permute-start.2 = (bf16[128,1024]{1,0:T(8,128)(2,1)S(1)}, bf16[128,1024]{1,0:T(8,128)(2,1)S(1)}, u32[]{:S(2)}, u32[]{:S(2)}) collective-permute-start(bf16[128,1024]{1,0:T(8,128)(2,1)S(1)} %get-tuple-element.62), channel_id=1, source_target_pairs={{0,24},{8,16},{16,8},{24,0},{1,25},{9,17},{17,9},{25,1},{2,26},{10... | collective-permute-start | bytes 786440 | tf_op jit(solution)/shard_map/ppermute | solution.py:165
  283.8 13.4 %copy-start.4 = (bf16[16,9216]{1,0:T(8,128)(2,1)S(1)}, bf16[16,9216]{1,0:T(8,128)(2,1)}, u32[]{:S(2)}) copy-start(bf16[16,9216]{1,0:T(8,128)(2,1)} %get-tuple-element.50) | copy-start | bytes 884740
  288.3 20.8 %copy-start.1 = (bf16[16,9216]{1,0:T(8,128)(2,1)S(1)}, bf16[16,9216]{1,0:T(8,128)(2,1)}, u32[]{:S(2)}) copy-start(bf16[16,9216]{1,0:T(8,128)(2,1)} %get-tuple-element.48) | copy-start | bytes 884740
  288.3 13.6 %all-to-all-start = ((bf16[8,64,512]{2,1,0:T(8,128)(2,1)}), bf16[8,64,512]{2,1,0:T(8,128)(2,1)S(1)}, u32[]{:S(2)}, u32[]{:S(2)}) async-start(bf16[8,64,512]{2,1,0:T(8,128)(2,1)} %get-tuple-element.46), calls=%async_computation | async-start | bytes 1048576 | tf_op jit(solution)/shard_map/all_to_all | solution.py:202
  292.2 18.3 %copy-start.6 = (bf16[16,3072]{1,0:T(8,128)(2,1)S(1)}, bf16[16,3072]{1,0:T(8,128)(2,1)}, u32[]{:S(2)}) copy-start(bf16[16,3072]{1,0:T(8,128)(2,1)} %get-tuple-element.55) | copy-start | bytes 294916
  292.2 18.3 %collective-permute-start.12 = (bf16[16,9216]{1,0:T(8,128)(2,1)S(1)}, bf16[16,9216]{1,0:T(8,128)(2,1)S(1)}, u32[]{:S(2)}, u32[]{:S(2)}) collective-permute-start(bf16[16,9216]{1,0:T(8,128)(2,1)S(1)} %copy-done.3), channel_id=1, source_target_pairs={{0,8},{8,0},{16,24},{24,16},{1,9},{9,1},{17,25},{25,17},{2,10},{10... | collective-permute-start | bytes 884744 | tf_op jit(solution)/shard_map/ppermute | solution.py:165
  297.2 23.6 %collective-permute-start.13 = (bf16[16,9216]{1,0:T(8,128)(2,1)S(1)}, bf16[16,9216]{1,0:T(8,128)(2,1)S(1)}, u32[]{:S(2)}, u32[]{:S(2)}) collective-permute-start(bf16[16,9216]{1,0:T(8,128)(2,1)S(1)} %copy-done.4), channel_id=1, source_target_pairs={{0,16},{8,24},{16,0},{24,8},{1,17},{9,25},{17,1},{25,9},{2,18},{10... | collective-permute-start | bytes 884744 | tf_op jit(solution)/shard_map/ppermute | solution.py:165
  297.5 23.3 %collective-permute-start.14 = (bf16[16,9216]{1,0:T(8,128)(2,1)}, bf16[16,9216]{1,0:T(8,128)(2,1)S(1)}, u32[]{:S(2)}, u32[]{:S(2)}) collective-permute-start(bf16[16,9216]{1,0:T(8,128)(2,1)} %get-tuple-element.51), channel_id=1, source_target_pairs={{0,24},{8,16},{16,8},{24,0},{1,25},{9,17},{17,9},{25,1},{2,26},{10... | collective-permute-start | bytes 884744 | tf_op jit(solution)/shard_map/ppermute | solution.py:165
  299.6 21.2 %collective-permute-start.15 = (bf16[16,3072]{1,0:T(8,128)(2,1)}, bf16[16,3072]{1,0:T(8,128)(2,1)}, u32[]{:S(2)}, u32[]{:S(2)}) collective-permute-start(bf16[16,3072]{1,0:T(8,128)(2,1)} %get-tuple-element.53), channel_id=1, source_target_pairs={{0,8},{8,0},{16,24},{24,16},{1,9},{9,1},{17,25},{25,17},{2,10},{10... | collective-permute-start | bytes 294920 | tf_op jit(solution)/shard_map/ppermute | solution.py:165
  300.6 33.4 %collective-permute-start.16 = (bf16[16,3072]{1,0:T(8,128)(2,1)}, bf16[16,3072]{1,0:T(8,128)(2,1)}, u32[]{:S(2)}, u32[]{:S(2)}) collective-permute-start(bf16[16,3072]{1,0:T(8,128)(2,1)} %get-tuple-element.54), channel_id=1, source_target_pairs={{0,16},{8,24},{16,0},{24,8},{1,17},{9,25},{17,1},{25,9},{2,18},{10... | collective-permute-start | bytes 294920 | tf_op jit(solution)/shard_map/ppermute | solution.py:165
  302.6 32.4 %all-to-all-start.1 = ((bf16[4,16,512]{2,1,0:T(8,128)(2,1)}), bf16[4,16,512]{2,1,0:T(8,128)(2,1)S(1)}, u32[]{:S(2)}, u32[]{:S(2)}) async-start(bf16[4,16,512]{2,1,0:T(8,128)(2,1)} %bitcast.11), calls=%async_computation.1 | async-start | bytes 131072 | tf_op jit(solution)/shard_map/all_to_all | solution.py:205
  309.1 11.7 %copy-start.2 = (bf16[16,3072]{1,0:T(8,128)(2,1)S(1)}, bf16[16,3072]{1,0:T(8,128)(2,1)}, u32[]{:S(2)}) copy-start(bf16[16,3072]{1,0:T(8,128)(2,1)} %get-tuple-element.52) | copy-start | bytes 294916
  310.4 24.6 %collective-permute-start.17 = (bf16[16,3072]{1,0:T(8,128)(2,1)S(1)}, bf16[16,3072]{1,0:T(8,128)(2,1)S(1)}, u32[]{:S(2)}, u32[]{:S(2)}) collective-permute-start(bf16[16,3072]{1,0:T(8,128)(2,1)S(1)} %copy-done.6), channel_id=1, source_target_pairs={{0,24},{8,16},{16,8},{24,0},{1,25},{9,17},{17,9},{25,1},{2,26},{10... | collective-permute-start | bytes 294920 | tf_op jit(solution)/shard_map/ppermute | solution.py:165
  (5 other events, 15.5 us)

commit v2 on v1

--- a/solution.py
+++ b/solution.py
@@ -28,7 +28,7 @@
 
 
 def chunk_kernel(
-    times, time_dev, count, first, last, carried, scale, source, where_ref, own_ref, *refs
+    times, time_dev, count, first, last, carried, scale, target, source, where_ref, own_ref, *refs
 ):
     recv_refs, refs = refs[: count - 1], refs[count - 1 :]
     root_ref, eig_ref, inv_ref = refs[:3]
@@ -80,14 +80,20 @@
             block_rows = times // (space_count * count)
             for s in range(space_count):
                 pieces = [
-                    total[pl.ds((i * space_count + s) * block_rows, block_rows), :]
+                    total[
+                        pl.ds(
+                            pl.multiple_of((target(me, i) * space_count + s) * block_rows, block_rows),
+                            block_rows,
+                        ),
+                        :,
+                    ]
                     for i in range(count)
                 ]
                 gram_ref[s] = (jnp.concatenate(pieces, axis=0) * scale).astype(jnp.bfloat16)
 
 
 def run_chunk(
-    snapshots, recv, root, eig, inv, prev, modes, where, span, group, tile, last, space_count, source
+    snapshots, recv, root, eig, inv, prev, modes, where, span, group, tile, last, space_count, target, source
 ):
     lo, hi = span
     group_lo, group_hi = group
@@ -99,7 +105,7 @@
     first = prev is None
     cells = snapshots.shape[1] * space_count
     kernel = functools.partial(
-        chunk_kernel, times, time_dev, count, first, last, len(modes), 1.0 / cells, source
+        chunk_kernel, times, time_dev, count, first, last, len(modes), 1.0 / cells, target, source
     )
     in_specs = [pl.BlockSpec((time_dev, tile), lambda g, w: (0, w[1] + lo + g))]
     in_specs += [pl.BlockSpec((time_dev, tile), lambda g, w: (0, g))] * (count - 1)
@@ -194,19 +200,22 @@
         pieces = groups[group][1] if group in groups else []
         pieces, gram = run_chunk(
             snapshots, received[n], root, eig, inv, gram, pieces, where,
-            (lo, hi), bounds, tile, last, space_count, source,
+            (lo, hi), bounds, tile, last, space_count, target, source,
         )
         groups[group] = (bounds[0], pieces)
 
     rows = gram.shape[1] // count
     parts = lax.all_to_all(gram, "space", split_axis=0, concat_axis=0, tiled=True)
-    row_sums = jnp.sum(parts.astype(jnp.float32), axis=0).astype(jnp.bfloat16)
-    row_sums = row_sums.reshape(count, rows, gram.shape[2])
-    parts = lax.all_to_all(row_sums, "tm", split_axis=0, concat_axis=0, tiled=True)
-    gram_rows = jnp.sum(parts.astype(jnp.float32), axis=0)
+    row_sums = [
+        jnp.sum(parts[:, s * rows : (s + 1) * rows].astype(jnp.float32), axis=0)
+        for s in range(count)
+    ]
+    gram_rows = row_sums[0]
+    for s in range(1, count):
+        gram_rows = gram_rows + permute(row_sums[s].astype(jnp.bfloat16), s).astype(jnp.float32)
 
     modes = jnp.zeros((depth, cell_dev), jnp.bfloat16)
-    modes, _ = lax.optimization_barrier((modes, row_sums))
+    modes, _ = lax.optimization_barrier((modes, row_sums[0]))
     for (lo, pieces) in groups.values():
         for s, piece in enumerate(pieces):
             if s > 0:

time: 337 us -> 339 us (level)
  starting transfers between devices: 48.2 us -> 54.4 us
    ppermute x18 -> x21, starting transfers between devices: 37.9 us -> 50.5 us  [permute(): return lax.ppermute(piece, 'tm', [(i, target(i, s)) for i in range(count)])]
    all_to_all x1 -> x0, starting transfers between devices: 6.4 us -> none  [local(): lax.all_to_all(row_sums, 'tm', split_axis=0, concat_axis=0, tiled=True)]
    ppermute x18 -> x21, waiting for transfers between devices: 236 us -> 235 us  [permute(): return lax.ppermute(piece, 'tm', [(i, target(i, s)) for i in range(count)])]
  transfers between devices with their start and end apart: 20 -> 22, of which waited for: 8 -> 9; matrix products, arithmetic and copies ran while one was open for 3% -> 2% of each run, Pallas kernels for 7% -> 7%
where the time goes in v2:
time: 339 us; the launch traced here: 338 us
  waiting for transfers between devices  235 us (69%)
  starting transfers between devices  54.4 us (16%)
  Pallas kernels  28.6 us (8%)
  local copies, waits for them, and re-layouts  17.3 us (5%)
    ppermute x21, waiting for transfers between devices, permute(): return lax.ppermute(piece, 'tm', [(i, target(i, s)) for i in range(count)])  235 us
    ppermute x21, starting transfers between devices, permute(): return lax.ppermute(piece, 'tm', [(i, target(i, s)) for i in range(count)])  50.5 us
    pallas_call x4, Pallas kernels, run_chunk(): pl.pallas_call(kernel, out_shape=out_shape, grid_spec=pltpu.PrefetchScala...  28.6 us
    dynamic_slice x6, local copies, waits for them, and re-layouts, local(): piece = lax.dynamic_slice_in_dim(base, start, (hi - lo) * tile, 1)  14.1 us
  transfers between devices with their start and end apart: 22, of which 9 were waited for; matrix products, arithmetic and copies ran while one was open for 2% of the time, Pallas kernels for 7%

profile of v2, /device:TPU:0, one launch (start us, length us, event | category | flops | bytes accessed | tf_op | source)
XLA Modules:
  0.0 338.3 jit_solution(4581481241187603687)
XLA Ops:
  5.0 5.5 %constant_dynamic-slice_fusion = (bf16[128,8192]{1,0:T(8,128)(2,1)S(1)}, bf16[128,8192]{1,0:T(8,128)(2,1)}, bf16[128,8192]{1,0:T(8,128)(2,1)}) fusion(bf16[128,49152]{1,0:T(8,128)(2,1)} %own_ref.7, s32[]{:T(128)S(6)} %select_n.81, s32[]{:T(128)S(6)} %select_n.80, s32[]{:T(128)S(6)} %select_n.79), kind=kLoop, calls=%fused_computation.19 | loop fusion | bytes 12582924 | tf_op jit(solution)/shard_map/dynamic_slice | solution.py:179
  10.5 3.1 collective-permute-start.6
  13.6 2.6 collective-permute-start.7
  17.1 3.5 %collective-permute-start.10 = (bf16[128,1024]{1,0:T(8,128)(2,1)}, bf16[128,1024]{1,0:T(8,128)(2,1)}, u32[]{:S(2)}, u32[]{:S(2)}) collective-permute-start(bf16[128,1024]{1,0:T(8,128)(2,1)} %constant_dynamic-slice_fusion.10), channel_id=1, source_target_pairs={{0,16},{8,24},{16,0},{24,8},{1,17},{9,25},{17,1},{25,9},{2,18},{10... | collective-permute-start | bytes 786440 | tf_op jit(solution)/shard_map/ppermute | solution.py:171
  20.5 2.3 constant_dynamic-slice_fusion.3
  23.5 131.9 %collective-permute-done.9.refs_0_ = bf16[128,1024]{1,0:T(8,128)(2,1)} collective-permute-done((bf16[128,1024]{1,0:T(8,128)(2,1)S(1)}, bf16[128,1024]{1,0:T(8,128)(2,1)}, u32[]{:S(2)}, u32[]{:S(2)}) %collective-permute-start.9) | collective-permute-done | bytes 262176 | tf_op jit(solution)/shard_map/ppermute | solution.py:171
  155.4 2.6 collective-permute-start.3
  160.0 48.0 %collective-permute-done.10.refs_1_ = bf16[128,1024]{1,0:T(8,128)(2,1)} collective-permute-done((bf16[128,1024]{1,0:T(8,128)(2,1)}, bf16[128,1024]{1,0:T(8,128)(2,1)}, u32[]{:S(2)}, u32[]{:S(2)}) %collective-permute-start.10) | collective-permute-done | bytes 262176 | tf_op jit(solution)/shard_map/ppermute | solution.py:171
  208.0 2.9 collective-permute-start.11
  212.9 4.3 %collective-permute-done.11.refs_2_ = bf16[128,1024]{1,0:T(8,128)(2,1)} collective-permute-done((bf16[128,1024]{1,0:T(8,128)(2,1)}, bf16[128,1024]{1,0:T(8,128)(2,1)}, u32[]{:S(2)}, u32[]{:S(2)}) %collective-permute-start.11) | collective-permute-done | bytes 262176 | tf_op jit(solution)/shard_map/ppermute | solution.py:171
  217.2 4.0 %collective-permute-start.4 = (bf16[128,2048]{1,0:T(8,128)(2,1)S(1)}, bf16[128,2048]{1,0:T(8,128)(2,1)}, u32[]{:S(2)}, u32[]{:S(2)}) collective-permute-start(bf16[128,2048]{1,0:T(8,128)(2,1)S(1)} %get-tuple-element.63), channel_id=1, source_target_pairs={{0,16},{8,24},{16,0},{24,8},{1,17},{9,25},{17,1},{25,9},{2,18},{10... | collective-permute-start | bytes 1572872 | tf_op jit(solution)/shard_map/ppermute | solution.py:171
  223.7 4.1 %chunk.3 = (bf16[16,9216]{1,0:T(8,128)(2,1)}, bf16[16,9216]{1,0:T(8,128)(2,1)}, bf16[16,9216]{1,0:T(8,128)(2,1)}, bf16[16,9216]{1,0:T(8,128)(2,1)}, f32[512,512]{1,0:T(8,128)}) custom-call(s32[2]{0:T(128)} %pad_add_fusion.where_ref, bf16[128,49152]{1,0:T(8,128)(2,1)} %own_ref.7, bf16[128,1024]{1,0:T(8,128)(2,1)} %collective-permute-done.9.refs_0_, ...), custom_call_target="tpu_custom_call" | custom-call | flops 603979776 | bytes 3145728 | tf_op jit(solution)/shard_map/chunk/pallas_call | solution.py:141
  227.9 2.6 collective-permute-start.1
  232.3 14.0 %chunk.4 = (bf16[16,9216]{1,0:T(8,128)(2,1)}, bf16[16,9216]{1,0:T(8,128)(2,1)}, bf16[16,9216]{1,0:T(8,128)(2,1)}, bf16[16,9216]{1,0:T(8,128)(2,1)}, f32[512,512]{1,0:T(8,128)}) custom-call(s32[2]{0:T(128)} %pad_add_fusion.where_ref, bf16[128,49152]{1,0:T(8,128)(2,1)} %own_ref.7, ...), custom_call_target="tpu_custom_call", output_to_operand_aliasing={{0}: (9, {}), {1}: (10, {}), {2}: (11, {}), {3}: (12, {})} | custom-call | flops 4831838208 | bytes 10485760 | tf_op jit(solution)/shard_map/chunk/pallas_call | solution.py:141
  246.3 19.9 %collective-permute-done.4.refs_1_ = bf16[128,2048]{1,0:T(8,128)(2,1)} collective-permute-done((bf16[128,2048]{1,0:T(8,128)(2,1)S(1)}, bf16[128,2048]{1,0:T(8,128)(2,1)}, u32[]{:S(2)}, u32[]{:S(2)}) %collective-permute-start.4) | collective-permute-done | bytes 524320 | tf_op jit(solution)/shard_map/ppermute | solution.py:171
  266.2 6.0 %chunk.5 = (bf16[16,3072]{1,0:T(8,128)(2,1)}, bf16[16,3072]{1,0:T(8,128)(2,1)}, bf16[16,3072]{1,0:T(8,128)(2,1)}, bf16[16,3072]{1,0:T(8,128)(2,1)}, f32[512,512]{1,0:T(8,128)}) custom-call(s32[2]{0:T(128)} %pad_add_fusion.where_ref, bf16[128,49152]{1,0:T(8,128)(2,1)} %own_ref.7, bf16[128,2048]{1,0:T(8,128)(2,1)} %collective-permute-done.3.refs_0_, ...), custom_call_target="tpu_custom_call" | custom-call | flops 1207959552 | bytes 4194304 | tf_op jit(solution)/shard_map/chunk/pallas_call | solution.py:141
  272.2 10.9 %collective-permute-done.1.refs_1_ = bf16[128,1024]{1,0:T(8,128)(2,1)} collective-permute-done((bf16[128,1024]{1,0:T(8,128)(2,1)}, bf16[128,1024]{1,0:T(8,128)(2,1)}, u32[]{:S(2)}, u32[]{:S(2)}) %collective-permute-start.1) | collective-permute-done | bytes 262176 | tf_op jit(solution)/shard_map/ppermute | solution.py:171
  283.8 4.5 %chunk_last.1 = (bf16[16,3072]{1,0:T(8,128)(2,1)}, bf16[16,3072]{1,0:T(8,128)(2,1)}, bf16[16,3072]{1,0:T(8,128)(2,1)}, bf16[16,3072]{1,0:T(8,128)(2,1)}, bf16[8,64,512]{2,1,0:T(8,128)(2,1)}) custom-call(s32[2]{0:T(128)} %pad_add_fusion.where_ref, ...), custom_call_target="tpu_custom_call", output_to_operand_aliasing={{0}: (9, {}), {1}: (10, {}), {2}: (11, {}), {3}: (12, {})} | custom-call | flops 603979776 | bytes 3145728 | tf_op jit(solution)/shard_map/chunk_last/pallas_call | solution.py:141
  288.3 3.9 %all-to-all-start = ((bf16[8,64,512]{2,1,0:T(8,128)(2,1)}), bf16[8,64,512]{2,1,0:T(8,128)(2,1)S(1)}, u32[]{:S(2)}, u32[]{:S(2)}) async-start(bf16[8,64,512]{2,1,0:T(8,128)(2,1)} %get-tuple-element.46), calls=%async_computation | async-start | bytes 1048576 | tf_op jit(solution)/shard_map/all_to_all | solution.py:208
  292.1 5.0 %collective-permute-start.15 = (bf16[16,9216]{1,0:T(8,128)(2,1)S(1)}, bf16[16,9216]{1,0:T(8,128)(2,1)S(1)}, u32[]{:S(2)}, u32[]{:S(2)}) collective-permute-start(bf16[16,9216]{1,0:T(8,128)(2,1)S(1)} %copy-done.3), channel_id=1, source_target_pairs={{0,8},{8,0},{16,24},{24,16},{1,9},{9,1},{17,25},{25,17},{2,10},{10... | collective-permute-start | bytes 884744 | tf_op jit(solution)/shard_map/ppermute | solution.py:171
  302.0 8.3 %collective-permute-done.15 = bf16[16,9216]{1,0:T(8,128)(2,1)S(1)} collective-permute-done((bf16[16,9216]{1,0:T(8,128)(2,1)S(1)}, bf16[16,9216]{1,0:T(8,128)(2,1)S(1)}, u32[]{:S(2)}, u32[]{:S(2)}) %collective-permute-start.15) | collective-permute-done | bytes 294944 | tf_op jit(solution)/shard_map/ppermute | solution.py:171
  312.5 8.4 %collective-permute-done.16 = bf16[16,9216]{1,0:T(8,128)(2,1)S(1)} collective-permute-done((bf16[16,9216]{1,0:T(8,128)(2,1)S(1)}, bf16[16,9216]{1,0:T(8,128)(2,1)S(1)}, u32[]{:S(2)}, u32[]{:S(2)}) %collective-permute-start.16) | collective-permute-done | bytes 294944 | tf_op jit(solution)/shard_map/ppermute | solution.py:171
  320.9 11.1 %collective-permute-start.13 = (bf16[16,512]{1,0:T(8,128)(2,1)S(1)}, bf16[16,512]{1,0:T(8,128)(2,1)S(1)}, u32[]{:S(2)}, u32[]{:S(2)}) collective-permute-start(bf16[16,512]{1,0:T(8,128)(2,1)S(1)} %get-tuple-element.58), channel_id=1, source_target_pairs={{0,16},{8,24},{16,0},{24,8},{1,17},{9,25},{17,1},{25,9},{2,18},{10... | collective-permute-start | bytes 49160 | tf_op jit(solution)/shard_map/ppermute | solution.py:171
  335.4 2.2 collective-permute-done.14
  (70 shorter events, 25.9 us)
Async XLA Ops:
  10.5 217.4 %collective-permute-start.6 = (bf16[128,8192]{1,0:T(8,128)(2,1)}, bf16[128,8192]{1,0:T(8,128)(2,1)}, u32[]{:S(2)}, u32[]{:S(2)}) collective-permute-start(bf16[128,8192]{1,0:T(8,128)(2,1)} %get-tuple-element.61), channel_id=1, source_target_pairs={{0,8},{8,0},{16,24},{24,16},{1,9},{9,1},{17,25},{25,17},{2,10},{10... | collective-permute-start | bytes 6291464 | tf_op jit(solution)/shard_map/ppermute | solution.py:171
  13.6 214.3 %collective-permute-start.7 = (bf16[128,8192]{1,0:T(8,128)(2,1)}, bf16[128,8192]{1,0:T(8,128)(2,1)}, u32[]{:S(2)}, u32[]{:S(2)}) collective-permute-start(bf16[128,8192]{1,0:T(8,128)(2,1)} %get-tuple-element.60), channel_id=1, source_target_pairs={{0,16},{8,24},{16,0},{24,8},{1,17},{9,25},{17,1},{25,9},{2,18},{10... | collective-permute-start | bytes 6291464 | tf_op jit(solution)/shard_map/ppermute | solution.py:171
  16.2 214.3 %collective-permute-start.8 = (bf16[128,8192]{1,0:T(8,128)(2,1)S(1)}, bf16[128,8192]{1,0:T(8,128)(2,1)}, u32[]{:S(2)}, u32[]{:S(2)}) collective-permute-start(bf16[128,8192]{1,0:T(8,128)(2,1)S(1)} %get-tuple-element.59), channel_id=1, source_target_pairs={{0,24},{8,16},{16,8},{24,0},{1,25},{9,17},{17,9},{25,1},{2,26},{10... | collective-permute-start | bytes 6291464 | tf_op jit(solution)/shard_map/ppermute | solution.py:171
  16.2 139.2 %collective-permute-start.9 = (bf16[128,1024]{1,0:T(8,128)(2,1)S(1)}, bf16[128,1024]{1,0:T(8,128)(2,1)}, u32[]{:S(2)}, u32[]{:S(2)}) collective-permute-start(bf16[128,1024]{1,0:T(8,128)(2,1)S(1)} %constant_dynamic-slice_fusion.9), channel_id=1, source_target_pairs={{0,8},{8,0},{16,24},{24,16},{1,9},{9,1},{17,25},{25,17},{2,10},{10... | collective-permute-start | bytes 786440 | tf_op jit(solution)/shard_map/ppermute | solution.py:171
  17.1 191.0 %collective-permute-start.10 = (bf16[128,1024]{1,0:T(8,128)(2,1)}, bf16[128,1024]{1,0:T(8,128)(2,1)}, u32[]{:S(2)}, u32[]{:S(2)}) collective-permute-start(bf16[128,1024]{1,0:T(8,128)(2,1)} %constant_dynamic-slice_fusion.10), channel_id=1, source_target_pairs={{0,16},{8,24},{16,0},{24,8},{1,17},{9,25},{17,1},{25,9},{2,18},{10... | collective-permute-start | bytes 786440 | tf_op jit(solution)/shard_map/ppermute | solution.py:171
  155.4 65.8 %collective-permute-start.3 = (bf16[128,2048]{1,0:T(8,128)(2,1)}, bf16[128,2048]{1,0:T(8,128)(2,1)}, u32[]{:S(2)}, u32[]{:S(2)}) collective-permute-start(bf16[128,2048]{1,0:T(8,128)(2,1)} %get-tuple-element.64), channel_id=1, source_target_pairs={{0,8},{8,0},{16,24},{24,16},{1,9},{9,1},{17,25},{25,17},{2,10},{10... | collective-permute-start | bytes 1572872 | tf_op jit(solution)/shard_map/ppermute | solution.py:171
  208.0 9.2 %collective-permute-start.11 = (bf16[128,1024]{1,0:T(8,128)(2,1)}, bf16[128,1024]{1,0:T(8,128)(2,1)}, u32[]{:S(2)}, u32[]{:S(2)}) collective-permute-start(bf16[128,1024]{1,0:T(8,128)(2,1)} %constant_dynamic-slice_fusion.11), channel_id=1, source_target_pairs={{0,24},{8,16},{16,8},{24,0},{1,25},{9,17},{17,9},{25,1},{2,26},{10... | collective-permute-start | bytes 786440 | tf_op jit(solution)/shard_map/ppermute | solution.py:171
  217.2 49.0 %collective-permute-start.4 = (bf16[128,2048]{1,0:T(8,128)(2,1)S(1)}, bf16[128,2048]{1,0:T(8,128)(2,1)}, u32[]{:S(2)}, u32[]{:S(2)}) collective-permute-start(bf16[128,2048]{1,0:T(8,128)(2,1)S(1)} %get-tuple-element.63), channel_id=1, source_target_pairs={{0,16},{8,24},{16,0},{24,8},{1,17},{9,25},{17,1},{25,9},{2,18},{10... | collective-permute-start | bytes 1572872 | tf_op jit(solution)/shard_map/ppermute | solution.py:171
  221.2 45.0 %collective-permute-start.5 = (bf16[128,2048]{1,0:T(8,128)(2,1)S(1)}, bf16[128,2048]{1,0:T(8,128)(2,1)}, u32[]{:S(2)}, u32[]{:S(2)}) collective-permute-start(bf16[128,2048]{1,0:T(8,128)(2,1)S(1)} %get-tuple-element.62), channel_id=1, source_target_pairs={{0,24},{8,16},{16,8},{24,0},{1,25},{9,17},{17,9},{25,1},{2,26},{10... | collective-permute-start | bytes 1572872 | tf_op jit(solution)/shard_map/ppermute | solution.py:171
  227.9 44.3 %collective-permute-start = (bf16[128,1024]{1,0:T(8,128)(2,1)}, bf16[128,1024]{1,0:T(8,128)(2,1)}, u32[]{:S(2)}, u32[]{:S(2)}) collective-permute-start(bf16[128,1024]{1,0:T(8,128)(2,1)} %get-tuple-element.67), channel_id=1, source_target_pairs={{0,8},{8,0},{16,24},{24,16},{1,9},{9,1},{17,25},{25,17},{2,10},{10... | collective-permute-start | bytes 786440 | tf_op jit(solution)/shard_map/ppermute | solution.py:171
  227.9 55.1 %collective-permute-start.1 = (bf16[128,1024]{1,0:T(8,128)(2,1)}, bf16[128,1024]{1,0:T(8,128)(2,1)}, u32[]{:S(2)}, u32[]{:S(2)}) collective-permute-start(bf16[128,1024]{1,0:T(8,128)(2,1)} %get-tuple-element.66), channel_id=1, source_target_pairs={{0,16},{8,24},{16,0},{24,8},{1,17},{9,25},{17,1},{25,9},{2,18},{10... | collective-permute-start | bytes 786440 | tf_op jit(solution)/shard_map/ppermute | solution.py:171
  230.5 52.5 %collective-permute-start.2 = (bf16[128,1024]{1,0:T(8,128)(2,1)S(1)}, bf16[128,1024]{1,0:T(8,128)(2,1)S(1)}, u32[]{:S(2)}, u32[]{:S(2)}) collective-permute-start(bf16[128,1024]{1,0:T(8,128)(2,1)S(1)} %get-tuple-element.65), channel_id=1, source_target_pairs={{0,24},{8,16},{16,8},{24,0},{1,25},{9,17},{17,9},{25,1},{2,26},{10... | collective-permute-start | bytes 786440 | tf_op jit(solution)/shard_map/ppermute | solution.py:171
  288.3 22.1 %copy-start.7 = (bf16[16,3072]{1,0:T(8,128)(2,1)S(1)}, bf16[16,3072]{1,0:T(8,128)(2,1)}, u32[]{:S(2)}) copy-start(bf16[16,3072]{1,0:T(8,128)(2,1)} %get-tuple-element.55) | copy-start | bytes 294916
  288.3 13.6 %all-to-all-start = ((bf16[8,64,512]{2,1,0:T(8,128)(2,1)}), bf16[8,64,512]{2,1,0:T(8,128)(2,1)S(1)}, u32[]{:S(2)}, u32[]{:S(2)}) async-start(bf16[8,64,512]{2,1,0:T(8,128)(2,1)} %get-tuple-element.46), calls=%async_computation | async-start | bytes 1048576 | tf_op jit(solution)/shard_map/all_to_all | solution.py:208
  292.1 18.2 %collective-permute-start.15 = (bf16[16,9216]{1,0:T(8,128)(2,1)S(1)}, bf16[16,9216]{1,0:T(8,128)(2,1)S(1)}, u32[]{:S(2)}, u32[]{:S(2)}) collective-permute-start(bf16[16,9216]{1,0:T(8,128)(2,1)S(1)} %copy-done.3), channel_id=1, source_target_pairs={{0,8},{8,0},{16,24},{24,16},{1,9},{9,1},{17,25},{25,17},{2,10},{10... | collective-permute-start | bytes 884744 | tf_op jit(solution)/shard_map/ppermute | solution.py:171
  297.1 23.7 %collective-permute-start.16 = (bf16[16,9216]{1,0:T(8,128)(2,1)S(1)}, bf16[16,9216]{1,0:T(8,128)(2,1)S(1)}, u32[]{:S(2)}, u32[]{:S(2)}) collective-permute-start(bf16[16,9216]{1,0:T(8,128)(2,1)S(1)} %copy-done.4), channel_id=1, source_target_pairs={{0,16},{8,24},{16,0},{24,8},{1,17},{9,25},{17,1},{25,9},{2,18},{10... | collective-permute-start | bytes 884744 | tf_op jit(solution)/shard_map/ppermute | solution.py:171
  297.4 23.4 %collective-permute-start.17 = (bf16[16,9216]{1,0:T(8,128)(2,1)S(1)}, bf16[16,9216]{1,0:T(8,128)(2,1)S(1)}, u32[]{:S(2)}, u32[]{:S(2)}) collective-permute-start(bf16[16,9216]{1,0:T(8,128)(2,1)S(1)} %copy-done.5), channel_id=1, source_target_pairs={{0,24},{8,16},{16,8},{24,0},{1,25},{9,17},{17,9},{25,1},{2,26},{10... | collective-permute-start | bytes 884744 | tf_op jit(solution)/shard_map/ppermute | solution.py:171
  299.6 32.4 %collective-permute-start.18 = (bf16[16,3072]{1,0:T(8,128)(2,1)}, bf16[16,3072]{1,0:T(8,128)(2,1)S(1)}, u32[]{:S(2)}, u32[]{:S(2)}) collective-permute-start(bf16[16,3072]{1,0:T(8,128)(2,1)} %get-tuple-element.53), channel_id=1, source_target_pairs={{0,8},{8,0},{16,24},{24,16},{1,9},{9,1},{17,25},{25,17},{2,10},{10... | collective-permute-start | bytes 294920 | tf_op jit(solution)/shard_map/ppermute | solution.py:171
  300.6 33.6 %collective-permute-start.19 = (bf16[16,3072]{1,0:T(8,128)(2,1)}, bf16[16,3072]{1,0:T(8,128)(2,1)S(1)}, u32[]{:S(2)}, u32[]{:S(2)}) collective-permute-start(bf16[16,3072]{1,0:T(8,128)(2,1)} %get-tuple-element.54), channel_id=1, source_target_pairs={{0,16},{8,24},{16,0},{24,8},{1,17},{9,25},{17,1},{25,9},{2,18},{10... | collective-permute-start | bytes 294920 | tf_op jit(solution)/shard_map/ppermute | solution.py:171
  302.0 30.0 %copy-start.2 = (bf16[16,3072]{1,0:T(8,128)(2,1)S(1)}, bf16[16,3072]{1,0:T(8,128)(2,1)}, u32[]{:S(2)}) copy-start(bf16[16,3072]{1,0:T(8,128)(2,1)} %get-tuple-element.52) | copy-start | bytes 294916
  310.4 23.9 %collective-permute-start.20 = (bf16[16,3072]{1,0:T(8,128)(2,1)S(1)}, bf16[16,3072]{1,0:T(8,128)(2,1)S(1)}, u32[]{:S(2)}, u32[]{:S(2)}) collective-permute-start(bf16[16,3072]{1,0:T(8,128)(2,1)S(1)} %copy-done.7), channel_id=1, source_target_pairs={{0,24},{8,16},{16,8},{24,0},{1,25},{9,17},{17,9},{25,1},{2,26},{10... | collective-permute-start | bytes 294920 | tf_op jit(solution)/shard_map/ppermute | solution.py:171
  320.8 13.5 %collective-permute-start.12 = (bf16[16,512]{1,0:T(8,128)(2,1)S(1)}, bf16[16,512]{1,0:T(8,128)(2,1)S(1)}, u32[]{:S(2)}, u32[]{:S(2)}) collective-permute-start(bf16[16,512]{1,0:T(8,128)(2,1)S(1)} %get-tuple-element.56), channel_id=1, source_target_pairs={{0,8},{8,0},{16,24},{24,16},{1,9},{9,1},{17,25},{25,17},{2,10},{10... | collective-permute-start | bytes 49160 | tf_op jit(solution)/shard_map/ppermute | solution.py:171
  320.9 14.6 %collective-permute-start.13 = (bf16[16,512]{1,0:T(8,128)(2,1)S(1)}, bf16[16,512]{1,0:T(8,128)(2,1)S(1)}, u32[]{:S(2)}, u32[]{:S(2)}) collective-permute-start(bf16[16,512]{1,0:T(8,128)(2,1)S(1)} %get-tuple-element.58), channel_id=1, source_target_pairs={{0,16},{8,24},{16,0},{24,8},{1,17},{9,25},{17,1},{25,9},{2,18},{10... | collective-permute-start | bytes 49160 | tf_op jit(solution)/shard_map/ppermute | solution.py:171
  332.0 5.6 %collective-permute-start.14 = (bf16[16,512]{1,0:T(8,128)(2,1)S(1)}, bf16[16,512]{1,0:T(8,128)(2,1)S(1)}, u32[]{:S(2)}, u32[]{:S(2)}) collective-permute-start(bf16[16,512]{1,0:T(8,128)(2,1)S(1)} %get-tuple-element.57), channel_id=1, source_target_pairs={{0,24},{8,16},{16,8},{24,0},{1,25},{9,17},{17,9},{25,1},{2,26},{10... | collective-permute-start | bytes 49160 | tf_op jit(solution)/shard_map/ppermute | solution.py:171
  (8 other events, 59.1 us)

commit v3 on v2

--- a/solution.py
+++ b/solution.py
@@ -172,13 +172,12 @@
 
     received = []
     base = snapshots
-    for n, (lo, hi, _) in enumerate(chunks):
+    for lo, hi, _ in chunks:
         pieces = {}
         for s in reversed(range(1, count)):
             start = target(me, s) * sub + lo * tile
             piece = lax.dynamic_slice_in_dim(base, start, (hi - lo) * tile, 1)
-            if n == 0:
-                base, piece = lax.optimization_barrier((base, piece))
+            base, piece = lax.optimization_barrier((base, piece))
             pieces[s] = permute(piece, s)
         received.append([pieces[s] for s in range(1, count)])
 
@@ -206,16 +205,29 @@
 
     rows = gram.shape[1] // count
     parts = lax.all_to_all(gram, "space", split_axis=0, concat_axis=0, tiled=True)
-    row_sums = [
-        jnp.sum(parts[:, s * rows : (s + 1) * rows].astype(jnp.float32), axis=0)
-        for s in range(count)
-    ]
-    gram_rows = row_sums[0]
-    for s in range(1, count):
-        gram_rows = gram_rows + permute(row_sums[s].astype(jnp.bfloat16), s).astype(jnp.float32)
+    held = {}
+    for s in range(count):
+        held[s] = jnp.sum(parts[:, s * rows : (s + 1) * rows].astype(jnp.float32), axis=0)
+    row_sums = held[0]
+    if count & (count - 1) == 0:
+        bit = 1
+        while bit < count:
+            moved = [s for s in held if s & bit]
+            packed = jnp.concatenate([held[s] for s in moved], axis=0).astype(jnp.bfloat16)
+            packed = permute(packed, bit).astype(jnp.float32)
+            for n, s in enumerate(moved):
+                held[s ^ bit] = held[s ^ bit] + packed[n * rows : (n + 1) * rows]
+                del held[s]
+            bit *= 2
+        gram_rows = held[0]
+    else:
+        gram_rows = held[0]
+        for s in range(1, count):
+            moved = permute(held[s].astype(jnp.bfloat16), s)
+            gram_rows = gram_rows + moved.astype(jnp.float32)
 
     modes = jnp.zeros((depth, cell_dev), jnp.bfloat16)
-    modes, _ = lax.optimization_barrier((modes, row_sums[0]))
+    modes, _ = lax.optimization_barrier((modes, row_sums))
     for (lo, pieces) in groups.values():
         for s, piece in enumerate(pieces):
             if s > 0:

time: 339 us -> 342 us (level)
  starting transfers between devices: 54.4 us -> 41.7 us
  waiting for transfers between devices: 235 us -> 243 us
  local copies, waits for them, and re-layouts: 17.3 us -> 24.6 us
    ppermute x21 -> x20, starting transfers between devices: 50.5 us -> 37.8 us  [permute(): return lax.ppermute(piece, 'tm', [(i, target(i, s)) for i in range(count)])]
    ppermute x21 -> x20, waiting for transfers between devices: 235 us -> 243 us  [permute(): return lax.ppermute(piece, 'tm', [(i, target(i, s)) for i in range(count)])]
    dynamic_slice x6 -> x12, local copies, waits for them, and re-layouts: 14.1 us -> 21.4 us  [local(): piece = lax.dynamic_slice_in_dim(base, start, (hi - lo) * tile, 1)]
  transfers between devices with their start and end apart: 22 -> 21, of which waited for: 9 -> 9; matrix products, arithmetic and copies ran while one was open for 2% -> 4% of each run, Pallas kernels for 7% -> 7%
where the time goes in v3:
time: 342 us; the launch traced here: 341 us
  waiting for transfers between devices  243 us (71%)
  starting transfers between devices  41.7 us (12%)
  Pallas kernels  28.8 us (8%)
  local copies, waits for them, and re-layouts  24.6 us (7%)
    ppermute x20, waiting for transfers between devices, permute(): return lax.ppermute(piece, 'tm', [(i, target(i, s)) for i in range(count)])  243 us
    ppermute x20, starting transfers between devices, permute(): return lax.ppermute(piece, 'tm', [(i, target(i, s)) for i in range(count)])  37.8 us
    pallas_call x4, Pallas kernels, run_chunk(): pl.pallas_call(kernel, out_shape=out_shape, grid_spec=pltpu.PrefetchScala...  28.8 us
    dynamic_slice x12, local copies, waits for them, and re-layouts, local(): piece = lax.dynamic_slice_in_dim(base, start, (hi - lo) * tile, 1)  21.4 us
  transfers between devices with their start and end apart: 21, of which 9 were waited for; matrix products, arithmetic and copies ran while one was open for 4% of the time, Pallas kernels for 7%

profile of v3, /device:TPU:0, one launch (start us, length us, event | category | flops | bytes accessed | tf_op | source)
XLA Modules:
  0.0 341.2 jit_solution(17231857587916348288)
XLA Ops:
  6.7 3.2 constant_dynamic-slice_fusion.7
  9.9 3.1 constant_dynamic-slice_fusion.6
  13.0 3.1 collective-permute-start.6
  16.1 2.6 collective-permute-start.7
  19.6 3.5 %collective-permute-start.10 = (bf16[128,1024]{1,0:T(8,128)(2,1)}, bf16[128,1024]{1,0:T(8,128)(2,1)}, u32[]{:S(2)}, u32[]{:S(2)}) collective-permute-start(bf16[128,1024]{1,0:T(8,128)(2,1)} %constant_dynamic-slice_fusion.10), channel_id=1, source_target_pairs={{0,16},{8,24},{16,0},{24,8},{1,17},{9,25},{17,1},{25,9},{2,18},{10... | collective-permute-start | bytes 786440 | tf_op jit(solution)/shard_map/ppermute | solution.py:171
  31.1 126.9 %collective-permute-done.9.refs_0_ = bf16[128,1024]{1,0:T(8,128)(2,1)} collective-permute-done((bf16[128,1024]{1,0:T(8,128)(2,1)}, bf16[128,1024]{1,0:T(8,128)(2,1)}, u32[]{:S(2)}, u32[]{:S(2)}) %collective-permute-start.9) | collective-permute-done | bytes 262176 | tf_op jit(solution)/shard_map/ppermute | solution.py:171
  158.0 2.5 collective-permute-start.3
  162.2 48.3 %collective-permute-done.10.refs_1_ = bf16[128,1024]{1,0:T(8,128)(2,1)} collective-permute-done((bf16[128,1024]{1,0:T(8,128)(2,1)}, bf16[128,1024]{1,0:T(8,128)(2,1)}, u32[]{:S(2)}, u32[]{:S(2)}) %collective-permute-start.10) | collective-permute-done | bytes 262176 | tf_op jit(solution)/shard_map/ppermute | solution.py:171
  210.5 3.1 collective-permute-start.11
  215.7 3.8 %collective-permute-done.11.refs_2_ = bf16[128,1024]{1,0:T(8,128)(2,1)} collective-permute-done((bf16[128,1024]{1,0:T(8,128)(2,1)S(1)}, bf16[128,1024]{1,0:T(8,128)(2,1)}, u32[]{:S(2)}, u32[]{:S(2)}) %collective-permute-start.11) | collective-permute-done | bytes 262176 | tf_op jit(solution)/shard_map/ppermute | solution.py:171
  219.5 4.6 %collective-permute-start.4 = (bf16[128,2048]{1,0:T(8,128)(2,1)S(1)}, bf16[128,2048]{1,0:T(8,128)(2,1)}, u32[]{:S(2)}, u32[]{:S(2)}) collective-permute-start(bf16[128,2048]{1,0:T(8,128)(2,1)S(1)} %constant_dynamic-slice_fusion.4), channel_id=1, source_target_pairs={{0,16},{8,24},{16,0},{24,8},{1,17},{9,25},{17,1},{25,9},{2,18},{10... | collective-permute-start | bytes 1572872 | tf_op jit(solution)/shard_map/ppermute | solution.py:171
  226.0 4.3 %chunk.3 = (bf16[16,9216]{1,0:T(8,128)(2,1)}, bf16[16,9216]{1,0:T(8,128)(2,1)}, bf16[16,9216]{1,0:T(8,128)(2,1)}, bf16[16,9216]{1,0:T(8,128)(2,1)}, f32[512,512]{1,0:T(8,128)}) custom-call(s32[2]{0:T(128)} %pad_add_fusion.where_ref, bf16[128,49152]{1,0:T(8,128)(2,1)} %own_ref.7, bf16[128,1024]{1,0:T(8,128)(2,1)} %collective-permute-done.9.refs_0_, ...), custom_call_target="tpu_custom_call" | custom-call | flops 603979776 | bytes 3145728 | tf_op jit(solution)/shard_map/chunk/pallas_call | solution.py:141
  230.3 3.2 collective-permute-start.1
  234.7 14.0 %chunk.4 = (bf16[16,9216]{1,0:T(8,128)(2,1)}, bf16[16,9216]{1,0:T(8,128)(2,1)}, bf16[16,9216]{1,0:T(8,128)(2,1)}, bf16[16,9216]{1,0:T(8,128)(2,1)}, f32[512,512]{1,0:T(8,128)}) custom-call(s32[2]{0:T(128)} %pad_add_fusion.where_ref, bf16[128,49152]{1,0:T(8,128)(2,1)} %own_ref.7, ...), custom_call_target="tpu_custom_call", output_to_operand_aliasing={{0}: (9, {}), {1}: (10, {}), {2}: (11, {}), {3}: (12, {})} | custom-call | flops 4831838208 | bytes 10485760 | tf_op jit(solution)/shard_map/chunk/pallas_call | solution.py:141
  248.7 19.6 %collective-permute-done.4.refs_1_ = bf16[128,2048]{1,0:T(8,128)(2,1)} collective-permute-done((bf16[128,2048]{1,0:T(8,128)(2,1)S(1)}, bf16[128,2048]{1,0:T(8,128)(2,1)}, u32[]{:S(2)}, u32[]{:S(2)}) %collective-permute-start.4) | collective-permute-done | bytes 524320 | tf_op jit(solution)/shard_map/ppermute | solution.py:171
  268.3 6.0 %chunk.5 = (bf16[16,3072]{1,0:T(8,128)(2,1)}, bf16[16,3072]{1,0:T(8,128)(2,1)}, bf16[16,3072]{1,0:T(8,128)(2,1)}, bf16[16,3072]{1,0:T(8,128)(2,1)}, f32[512,512]{1,0:T(8,128)}) custom-call(s32[2]{0:T(128)} %pad_add_fusion.where_ref, bf16[128,49152]{1,0:T(8,128)(2,1)} %own_ref.7, bf16[128,2048]{1,0:T(8,128)(2,1)} %collective-permute-done.3.refs_0_, ...), custom_call_target="tpu_custom_call" | custom-call | flops 1207959552 | bytes 4194304 | tf_op jit(solution)/shard_map/chunk/pallas_call | solution.py:141
  274.3 10.9 %collective-permute-done.1.refs_1_ = bf16[128,1024]{1,0:T(8,128)(2,1)} collective-permute-done((bf16[128,1024]{1,0:T(8,128)(2,1)}, bf16[128,1024]{1,0:T(8,128)(2,1)}, u32[]{:S(2)}, u32[]{:S(2)}) %collective-permute-start.1) | collective-permute-done | bytes 262176 | tf_op jit(solution)/shard_map/ppermute | solution.py:171
  285.9 4.5 %chunk_last.1 = (bf16[16,3072]{1,0:T(8,128)(2,1)}, bf16[16,3072]{1,0:T(8,128)(2,1)}, bf16[16,3072]{1,0:T(8,128)(2,1)}, bf16[16,3072]{1,0:T(8,128)(2,1)}, bf16[8,64,512]{2,1,0:T(8,128)(2,1)}) custom-call(s32[2]{0:T(128)} %pad_add_fusion.where_ref, ...), custom_call_target="tpu_custom_call", output_to_operand_aliasing={{0}: (9, {}), {1}: (10, {}), {2}: (11, {}), {3}: (12, {})} | custom-call | flops 603979776 | bytes 3145728 | tf_op jit(solution)/shard_map/chunk_last/pallas_call | solution.py:141
  290.4 3.9 %all-to-all-start = ((bf16[8,64,512]{2,1,0:T(8,128)(2,1)}), bf16[8,64,512]{2,1,0:T(8,128)(2,1)S(1)}, u32[]{:S(2)}, u32[]{:S(2)}) async-start(bf16[8,64,512]{2,1,0:T(8,128)(2,1)} %get-tuple-element.80), calls=%async_computation | async-start | bytes 1048576 | tf_op jit(solution)/shard_map/all_to_all | solution.py:207
  294.3 5.5 %collective-permute-start.14 = (bf16[16,9216]{1,0:T(8,128)(2,1)S(1)}, bf16[16,9216]{1,0:T(8,128)(2,1)S(1)}, u32[]{:S(2)}, u32[]{:S(2)}) collective-permute-start(bf16[16,9216]{1,0:T(8,128)(2,1)S(1)} %copy-done.3), channel_id=1, source_target_pairs={{0,8},{8,0},{16,24},{24,16},{1,9},{9,1},{17,25},{25,17},{2,10},{10... | collective-permute-start | bytes 884744 | tf_op jit(solution)/shard_map/ppermute | solution.py:171
  304.6 8.4 %collective-permute-done.14 = bf16[16,9216]{1,0:T(8,128)(2,1)S(1)} collective-permute-done((bf16[16,9216]{1,0:T(8,128)(2,1)S(1)}, bf16[16,9216]{1,0:T(8,128)(2,1)S(1)}, u32[]{:S(2)}, u32[]{:S(2)}) %collective-permute-start.14) | collective-permute-done | bytes 294944 | tf_op jit(solution)/shard_map/ppermute | solution.py:171
  315.0 8.5 %collective-permute-done.15 = bf16[16,9216]{1,0:T(8,128)(2,1)S(1)} collective-permute-done((bf16[16,9216]{1,0:T(8,128)(2,1)S(1)}, bf16[16,9216]{1,0:T(8,128)(2,1)S(1)}, u32[]{:S(2)}, u32[]{:S(2)}) %collective-permute-start.15) | collective-permute-done | bytes 294944 | tf_op jit(solution)/shard_map/ppermute | solution.py:171
  323.6 12.2 %collective-permute-done.18 = bf16[16,3072]{1,0:T(8,128)(2,1)S(1)} collective-permute-done((bf16[16,3072]{1,0:T(8,128)(2,1)}, bf16[16,3072]{1,0:T(8,128)(2,1)S(1)}, u32[]{:S(2)}, u32[]{:S(2)}) %collective-permute-start.18) | collective-permute-done | bytes 98336 | tf_op jit(solution)/shard_map/ppermute | solution.py:171
  336.0 4.6 %collective-permute-done.13 = bf16[16,512]{1,0:T(8,128)(2,1)S(1)} collective-permute-done((bf16[16,512]{1,0:T(8,128)(2,1)S(1)}, bf16[16,512]{1,0:T(8,128)(2,1)S(1)}, u32[]{:S(2)}, u32[]{:S(2)}) %collective-permute-start.13) | collective-permute-done | bytes 16416 | tf_op jit(solution)/shard_map/ppermute | solution.py:171
  (79 shorter events, 30.3 us)
Async XLA Ops:
  13.0 217.3 %collective-permute-start.6 = (bf16[128,8192]{1,0:T(8,128)(2,1)}, bf16[128,8192]{1,0:T(8,128)(2,1)}, u32[]{:S(2)}, u32[]{:S(2)}) collective-permute-start(bf16[128,8192]{1,0:T(8,128)(2,1)} %constant_dynamic-slice_fusion.6), channel_id=1, source_target_pairs={{0,8},{8,0},{16,24},{24,16},{1,9},{9,1},{17,25},{25,17},{2,10},{10... | collective-permute-start | bytes 6291464 | tf_op jit(solution)/shard_map/ppermute | solution.py:171
  16.1 214.2 %collective-permute-start.7 = (bf16[128,8192]{1,0:T(8,128)(2,1)}, bf16[128,8192]{1,0:T(8,128)(2,1)}, u32[]{:S(2)}, u32[]{:S(2)}) collective-permute-start(bf16[128,8192]{1,0:T(8,128)(2,1)} %constant_dynamic-slice_fusion.7), channel_id=1, source_target_pairs={{0,16},{8,24},{16,0},{24,8},{1,17},{9,25},{17,1},{25,9},{2,18},{10... | collective-permute-start | bytes 6291464 | tf_op jit(solution)/shard_map/ppermute | solution.py:171
  18.7 214.9 %collective-permute-start.8 = (bf16[128,8192]{1,0:T(8,128)(2,1)S(1)}, bf16[128,8192]{1,0:T(8,128)(2,1)}, u32[]{:S(2)}, u32[]{:S(2)}) collective-permute-start(bf16[128,8192]{1,0:T(8,128)(2,1)S(1)} %constant_dynamic-slice_fusion.8), channel_id=1, source_target_pairs={{0,24},{8,16},{16,8},{24,0},{1,25},{9,17},{17,9},{25,1},{2,26},{10... | collective-permute-start | bytes 6291464 | tf_op jit(solution)/shard_map/ppermute | solution.py:171
  18.7 139.3 %collective-permute-start.9 = (bf16[128,1024]{1,0:T(8,128)(2,1)}, bf16[128,1024]{1,0:T(8,128)(2,1)}, u32[]{:S(2)}, u32[]{:S(2)}) collective-permute-start(bf16[128,1024]{1,0:T(8,128)(2,1)} %constant_dynamic-slice_fusion.9), channel_id=1, source_target_pairs={{0,8},{8,0},{16,24},{24,16},{1,9},{9,1},{17,25},{25,17},{2,10},{10... | collective-permute-start | bytes 786440 | tf_op jit(solution)/shard_map/ppermute | solution.py:171
  19.6 191.0 %collective-permute-start.10 = (bf16[128,1024]{1,0:T(8,128)(2,1)}, bf16[128,1024]{1,0:T(8,128)(2,1)}, u32[]{:S(2)}, u32[]{:S(2)}) collective-permute-start(bf16[128,1024]{1,0:T(8,128)(2,1)} %constant_dynamic-slice_fusion.10), channel_id=1, source_target_pairs={{0,16},{8,24},{16,0},{24,8},{1,17},{9,25},{17,1},{25,9},{2,18},{10... | collective-permute-start | bytes 786440 | tf_op jit(solution)/shard_map/ppermute | solution.py:171
  158.0 66.1 %collective-permute-start.3 = (bf16[128,2048]{1,0:T(8,128)(2,1)}, bf16[128,2048]{1,0:T(8,128)(2,1)}, u32[]{:S(2)}, u32[]{:S(2)}) collective-permute-start(bf16[128,2048]{1,0:T(8,128)(2,1)} %constant_dynamic-slice_fusion.3), channel_id=1, source_target_pairs={{0,8},{8,0},{16,24},{24,16},{1,9},{9,1},{17,25},{25,17},{2,10},{10... | collective-permute-start | bytes 1572872 | tf_op jit(solution)/shard_map/ppermute | solution.py:171
  210.5 9.0 %collective-permute-start.11 = (bf16[128,1024]{1,0:T(8,128)(2,1)S(1)}, bf16[128,1024]{1,0:T(8,128)(2,1)}, u32[]{:S(2)}, u32[]{:S(2)}) collective-permute-start(bf16[128,1024]{1,0:T(8,128)(2,1)S(1)} %constant_dynamic-slice_fusion.11), channel_id=1, source_target_pairs={{0,24},{8,16},{16,8},{24,0},{1,25},{9,17},{17,9},{25,1},{2,26},{10... | collective-permute-start | bytes 786440 | tf_op jit(solution)/shard_map/ppermute | solution.py:171
  219.5 48.8 %collective-permute-start.4 = (bf16[128,2048]{1,0:T(8,128)(2,1)S(1)}, bf16[128,2048]{1,0:T(8,128)(2,1)}, u32[]{:S(2)}, u32[]{:S(2)}) collective-permute-start(bf16[128,2048]{1,0:T(8,128)(2,1)S(1)} %constant_dynamic-slice_fusion.4), channel_id=1, source_target_pairs={{0,16},{8,24},{16,0},{24,8},{1,17},{9,25},{17,1},{25,9},{2,18},{10... | collective-permute-start | bytes 1572872 | tf_op jit(solution)/shard_map/ppermute | solution.py:171
  224.1 44.2 %collective-permute-start.5 = (bf16[128,2048]{1,0:T(8,128)(2,1)S(1)}, bf16[128,2048]{1,0:T(8,128)(2,1)}, u32[]{:S(2)}, u32[]{:S(2)}) collective-permute-start(bf16[128,2048]{1,0:T(8,128)(2,1)S(1)} %constant_dynamic-slice_fusion.5), channel_id=1, source_target_pairs={{0,24},{8,16},{16,8},{24,0},{1,25},{9,17},{17,9},{25,1},{2,26},{10... | collective-permute-start | bytes 1572872 | tf_op jit(solution)/shard_map/ppermute | solution.py:171
  230.3 44.0 %collective-permute-start = (bf16[128,1024]{1,0:T(8,128)(2,1)}, bf16[128,1024]{1,0:T(8,128)(2,1)}, u32[]{:S(2)}, u32[]{:S(2)}) collective-permute-start(bf16[128,1024]{1,0:T(8,128)(2,1)} %constant_dynamic-slice_fusion), channel_id=1, source_target_pairs={{0,8},{8,0},{16,24},{24,16},{1,9},{9,1},{17,25},{25,17},{2,10},{10... | collective-permute-start | bytes 786440 | tf_op jit(solution)/shard_map/ppermute | solution.py:171
  230.3 54.8 %collective-permute-start.1 = (bf16[128,1024]{1,0:T(8,128)(2,1)}, bf16[128,1024]{1,0:T(8,128)(2,1)}, u32[]{:S(2)}, u32[]{:S(2)}) collective-permute-start(bf16[128,1024]{1,0:T(8,128)(2,1)} %constant_dynamic-slice_fusion.1), channel_id=1, source_target_pairs={{0,16},{8,24},{16,0},{24,8},{1,17},{9,25},{17,1},{25,9},{2,18},{10... | collective-permute-start | bytes 786440 | tf_op jit(solution)/shard_map/ppermute | solution.py:171
  233.5 51.6 %collective-permute-start.2 = (bf16[128,1024]{1,0:T(8,128)(2,1)S(1)}, bf16[128,1024]{1,0:T(8,128)(2,1)S(1)}, u32[]{:S(2)}, u32[]{:S(2)}) collective-permute-start(bf16[128,1024]{1,0:T(8,128)(2,1)S(1)} %copy-done.6), channel_id=1, source_target_pairs={{0,24},{8,16},{16,8},{24,0},{1,25},{9,17},{17,9},{25,1},{2,26},{10... | collective-permute-start | bytes 786440 | tf_op jit(solution)/shard_map/ppermute | solution.py:171
  290.4 14.1 %copy-start.1 = (bf16[16,9216]{1,0:T(8,128)(2,1)S(1)}, bf16[16,9216]{1,0:T(8,128)(2,1)}, u32[]{:S(2)}) copy-start(bf16[16,9216]{1,0:T(8,128)(2,1)} %get-tuple-element.82) | copy-start | bytes 884740
  290.4 22.5 %copy-start.8 = (bf16[16,3072]{1,0:T(8,128)(2,1)S(1)}, bf16[16,3072]{1,0:T(8,128)(2,1)}, u32[]{:S(2)}) copy-start(bf16[16,3072]{1,0:T(8,128)(2,1)} %get-tuple-element.89) | copy-start | bytes 294916
  290.4 14.0 %all-to-all-start = ((bf16[8,64,512]{2,1,0:T(8,128)(2,1)}), bf16[8,64,512]{2,1,0:T(8,128)(2,1)S(1)}, u32[]{:S(2)}, u32[]{:S(2)}) async-start(bf16[8,64,512]{2,1,0:T(8,128)(2,1)} %get-tuple-element.80), calls=%async_computation | async-start | bytes 1048576 | tf_op jit(solution)/shard_map/all_to_all | solution.py:207
  294.3 18.7 %collective-permute-start.14 = (bf16[16,9216]{1,0:T(8,128)(2,1)S(1)}, bf16[16,9216]{1,0:T(8,128)(2,1)S(1)}, u32[]{:S(2)}, u32[]{:S(2)}) collective-permute-start(bf16[16,9216]{1,0:T(8,128)(2,1)S(1)} %copy-done.3), channel_id=1, source_target_pairs={{0,8},{8,0},{16,24},{24,16},{1,9},{9,1},{17,25},{25,17},{2,10},{10... | collective-permute-start | bytes 884744 | tf_op jit(solution)/shard_map/ppermute | solution.py:171
  299.7 23.7 %collective-permute-start.15 = (bf16[16,9216]{1,0:T(8,128)(2,1)S(1)}, bf16[16,9216]{1,0:T(8,128)(2,1)S(1)}, u32[]{:S(2)}, u32[]{:S(2)}) collective-permute-start(bf16[16,9216]{1,0:T(8,128)(2,1)S(1)} %copy-done.4), channel_id=1, source_target_pairs={{0,16},{8,24},{16,0},{24,8},{1,17},{9,25},{17,1},{25,9},{2,18},{10... | collective-permute-start | bytes 884744 | tf_op jit(solution)/shard_map/ppermute | solution.py:171
  300.0 23.5 %collective-permute-start.16 = (bf16[16,9216]{1,0:T(8,128)(2,1)S(1)}, bf16[16,9216]{1,0:T(8,128)(2,1)S(1)}, u32[]{:S(2)}, u32[]{:S(2)}) collective-permute-start(bf16[16,9216]{1,0:T(8,128)(2,1)S(1)} %copy-done.5), channel_id=1, source_target_pairs={{0,24},{8,16},{16,8},{24,0},{1,25},{9,17},{17,9},{25,1},{2,26},{10... | collective-permute-start | bytes 884744 | tf_op jit(solution)/shard_map/ppermute | solution.py:171
  302.2 21.4 %collective-permute-start.17 = (bf16[16,3072]{1,0:T(8,128)(2,1)}, bf16[16,3072]{1,0:T(8,128)(2,1)S(1)}, u32[]{:S(2)}, u32[]{:S(2)}) collective-permute-start(bf16[16,3072]{1,0:T(8,128)(2,1)} %get-tuple-element.87), channel_id=1, source_target_pairs={{0,8},{8,0},{16,24},{24,16},{1,9},{9,1},{17,25},{25,17},{2,10},{10... | collective-permute-start | bytes 294920 | tf_op jit(solution)/shard_map/ppermute | solution.py:171
  303.2 32.6 %collective-permute-start.18 = (bf16[16,3072]{1,0:T(8,128)(2,1)}, bf16[16,3072]{1,0:T(8,128)(2,1)S(1)}, u32[]{:S(2)}, u32[]{:S(2)}) collective-permute-start(bf16[16,3072]{1,0:T(8,128)(2,1)} %get-tuple-element.88), channel_id=1, source_target_pairs={{0,16},{8,24},{16,0},{24,8},{1,17},{9,25},{17,1},{25,9},{2,18},{10... | collective-permute-start | bytes 294920 | tf_op jit(solution)/shard_map/ppermute | solution.py:171
  304.5 19.0 %copy-start.2 = (bf16[16,3072]{1,0:T(8,128)(2,1)S(1)}, bf16[16,3072]{1,0:T(8,128)(2,1)}, u32[]{:S(2)}) copy-start(bf16[16,3072]{1,0:T(8,128)(2,1)} %get-tuple-element.86) | copy-start | bytes 294916
  312.9 23.0 %collective-permute-start.19 = (bf16[16,3072]{1,0:T(8,128)(2,1)S(1)}, bf16[16,3072]{1,0:T(8,128)(2,1)S(1)}, u32[]{:S(2)}, u32[]{:S(2)}) collective-permute-start(bf16[16,3072]{1,0:T(8,128)(2,1)S(1)} %copy-done.8), channel_id=1, source_target_pairs={{0,24},{8,16},{16,8},{24,0},{1,25},{9,17},{17,9},{25,1},{2,26},{10... | collective-permute-start | bytes 294920 | tf_op jit(solution)/shard_map/ppermute | solution.py:171
  323.5 12.4 %collective-permute-start.12 = (bf16[32,512]{1,0:T(8,128)(2,1)S(1)}, bf16[32,512]{1,0:T(8,128)(2,1)S(1)}, u32[]{:S(2)}, u32[]{:S(2)}) collective-permute-start(bf16[32,512]{1,0:T(8,128)(2,1)S(1)} %pad_maximum_fusion.1), channel_id=1, source_target_pairs={{0,8},{8,0},{16,24},{24,16},{1,9},{9,1},{17,25},{25,17},{2,10},{10... | collective-permute-start | bytes 98312 | tf_op jit(solution)/shard_map/ppermute | solution.py:171
  335.9 4.7 %collective-permute-start.13 = (bf16[16,512]{1,0:T(8,128)(2,1)S(1)}, bf16[16,512]{1,0:T(8,128)(2,1)S(1)}, u32[]{:S(2)}, u32[]{:S(2)}) collective-permute-start(bf16[16,512]{1,0:T(8,128)(2,1)S(1)} %fusion), channel_id=1, source_target_pairs={{0,16},{8,24},{16,0},{24,8},{1,17},{9,25},{17,1},{25,9},{2,18},{10... | collective-permute-start | bytes 49160 | tf_op jit(solution)/shard_map/ppermute | solution.py:171
  (8 other events, 61.4 us)
